TPU v7x, 128 devices: a whole 4x4x4 slice. The times are simulated.
128 devices in a mesh: frame: 16 (over x, y), pack: 8 (over z, core).
Axes of the slice: x: 4, y: 4, z: 4, core: 2. Of those that a mesh axis runs over, the one named last changes fastest.
Arguments:
- inputs: bfloat16 [16, 4096, 2240], P('frame', 'pack'), may hold values from -9 to 9
- weight: bfloat16 [2240, 3360], replicated, may hold values from -0.125 to 0.125
- clip_of_row: int32 [16, 4096], P('frame', 'pack'), may hold values from 0 to 1, as said below
- out_grad: bfloat16 [16, 4096, 1120], P('frame', 'pack'), may hold values from -6 to 6
Outputs:
- attention_out: bfloat16 [16, 4096, 1120], P('frame', 'pack')
- input_grad: bfloat16 [16, 4096, 2240], P('frame', 'pack')
Inputs may be any that keep to these rules, and one draw needn't show every extreme that they name: `clip_of_row`: each device holds at most 384 rows of one clip, hence at least 128 rows of each; some device holds exactly 384 rows of clip 0 and another exactly 384 rows of clip 1; the number of rows of a clip on a device is the same for every frame index; rows of a device are in no particular order.
All inputs are finite; a program needn't handle non-finite values.
Results may differ from a plain program's by a relative error of at most 0.034.
Values may be sent and summed in bfloat16 or wider, within the bound.
A program may use at most 128 MiB of HBM per device.

v0:
```python
import jax
import jax.numpy as jnp
from jax import lax
from jax.sharding import PartitionSpec as P

HEAD = 112
CLIPS = 2
CAP = 384


EPS = 1e-06


def carried_in(part, axis, combine, identity, reverse):
    count = lax.axis_size(axis)
    place = lax.axis_index(axis)
    ahead = count - 1 - place if reverse else place
    gathered = jax.tree.map(lambda a: lax.all_gather(a, axis), part)
    state = jax.tree.map(lambda a, e: jnp.zeros_like(a) + jnp.asarray(e, a.dtype), part, identity)

    def one(hop, state):
        source = count - 1 - hop if reverse else hop
        return combine(
            state, jax.tree.map(lambda a: lax.dynamic_index_in_dim(a, source, 0, False), gathered)
        )

    return lax.fori_loop(0, ahead, one, state)


def add_pair(earlier, later):
    return (earlier[0] + later[0], earlier[1] + later[1])


def block_terms(feat_slots):
    clip_count, slot_count, triple = feat_slots.shape
    head_count = triple // (3 * HEAD)
    split_parts = feat_slots.reshape(clip_count, slot_count, 3, head_count, HEAD)
    key_part = split_parts[:, :, 1]
    value_part = split_parts[:, :, 2]
    block_state = jnp.einsum(
        "cshd,cshe->chde", key_part, value_part, preferred_element_type=jnp.float32
    )
    block_norm = jnp.sum(key_part, axis=1, dtype=jnp.float32)
    return (block_state, block_norm)


def query_terms(feat_slots, state_lo, norm_lo, grad_slots):
    clip_count, slot_count, triple = feat_slots.shape
    inner_width = triple // 3
    head_count = inner_width // HEAD
    split_parts = feat_slots.reshape(clip_count, slot_count, 3, head_count, HEAD)
    query_part = split_parts[:, :, 0]
    numerator = jnp.einsum(
        "cshd,chde->cshe", query_part, state_lo, preferred_element_type=jnp.float32
    )
    query_wide = query_part.astype(jnp.float32)
    denominator = jnp.sum(query_wide * norm_lo.astype(jnp.float32)[:, None], axis=-1) + EPS
    attended = numerator / denominator[..., None]
    cotangent = grad_slots.reshape(clip_count, slot_count, head_count, HEAD).astype(jnp.float32)
    numer_grad = (cotangent / denominator[..., None]).astype(jnp.bfloat16)
    denom_grad = -jnp.sum(cotangent * attended, axis=-1) / denominator
    grad_block = jnp.einsum(
        "cshd,cshe->chde", query_part, numer_grad, preferred_element_type=jnp.float32
    )
    dnorm_block = jnp.sum(denom_grad[..., None] * query_wide, axis=1)
    out_slots = attended.astype(jnp.bfloat16).reshape(clip_count, slot_count, inner_width)
    return (out_slots, numer_grad, denom_grad, grad_block, dnorm_block)


def back_terms(feat_slots, numer_grad, denom_grad, state_lo, norm_lo, grad_lo, dnorm_lo):
    clip_count, slot_count, triple = feat_slots.shape
    head_count = triple // (3 * HEAD)
    split_parts = feat_slots.reshape(clip_count, slot_count, 3, head_count, HEAD)
    query_part = split_parts[:, :, 0]
    key_part = split_parts[:, :, 1]
    value_part = split_parts[:, :, 2]
    query_grad = jnp.einsum(
        "cshe,chde->cshd", numer_grad, state_lo, preferred_element_type=jnp.float32
    )
    query_grad = query_grad + denom_grad[..., None] * norm_lo.astype(jnp.float32)[:, None]
    query_grad = jnp.where(query_part > 0, query_grad, 0.0)
    key_grad = jnp.einsum(
        "cshe,chde->cshd", value_part, grad_lo, preferred_element_type=jnp.float32
    )
    key_grad = key_grad + dnorm_lo.astype(jnp.float32)[:, None]
    key_grad = jnp.where(key_part > 0, key_grad, 0.0)
    value_grad = jnp.einsum(
        "cshd,chde->cshe", key_part, grad_lo, preferred_element_type=jnp.float32
    )
    stacked = jnp.stack([query_grad, key_grad, value_grad], axis=2).astype(jnp.bfloat16)
    return stacked.reshape(clip_count, slot_count, triple)


def per_device(inputs, weight, clip_of_row, out_grad):
    inner_width = out_grad.shape[2]
    clip_count = CLIPS
    capacity = CAP
    projected = jnp.dot(inputs[0], weight, preferred_element_type=jnp.float32)
    features = jnp.concatenate(
        [jax.nn.relu(projected[:, : 2 * inner_width]), projected[:, 2 * inner_width :]], axis=1
    )
    features = features.astype(jnp.bfloat16)
    labels = clip_of_row[0]
    onehot = (labels[:, None] == jnp.arange(clip_count, dtype=jnp.int32)[None, :]).astype(jnp.int32)
    rank_in_clip = jnp.sum((jnp.cumsum(onehot, axis=0) - 1) * onehot, axis=1)
    slot_index = labels * capacity + rank_in_clip
    feat_slots = (
        jnp.zeros((clip_count * capacity, 3 * inner_width), jnp.bfloat16)
        .at[slot_index]
        .set(features)
    )
    feat_slots = feat_slots.reshape(clip_count, capacity, 3 * inner_width)
    grad_slots = (
        jnp.zeros((clip_count * capacity, inner_width), jnp.bfloat16)
        .at[slot_index]
        .set(out_grad[0])
    )
    grad_slots = grad_slots.reshape(clip_count, capacity, inner_width)
    local_state, local_norm = block_terms(feat_slots)
    block_state, block_norm = lax.psum((local_state, local_norm), "pack")
    earlier_state, earlier_norm = carried_in(
        (block_state, block_norm),
        "frame",
        add_pair,
        (jnp.zeros_like(block_state), jnp.zeros_like(block_norm)),
        False,
    )
    state_lo = (earlier_state + block_state).astype(jnp.bfloat16)
    norm_lo = (earlier_norm + block_norm).astype(jnp.bfloat16)
    out_slots, numer_grad, denom_grad, local_grad, local_dnorm = query_terms(
        feat_slots, state_lo, norm_lo, grad_slots
    )
    grad_block, dnorm_block = lax.psum((local_grad, local_dnorm), "pack")
    later_grad, later_dnorm = carried_in(
        (grad_block, dnorm_block),
        "frame",
        add_pair,
        (jnp.zeros_like(grad_block), jnp.zeros_like(dnorm_block)),
        True,
    )
    grad_lo = (later_grad + grad_block).astype(jnp.bfloat16)
    dnorm_lo = (later_dnorm + dnorm_block).astype(jnp.bfloat16)
    feat_grads = back_terms(
        feat_slots, numer_grad, denom_grad, state_lo, norm_lo, grad_lo, dnorm_lo
    )
    attention_rows = out_slots.reshape(clip_count * capacity, inner_width)[slot_index]
    grad_rows = feat_grads.reshape(clip_count * capacity, 3 * inner_width)[slot_index]
    input_grad = jnp.einsum(
        "tk,dk->td", grad_rows, weight, preferred_element_type=jnp.float32
    ).astype(jnp.bfloat16)
    return (attention_rows[None], input_grad[None])


def solution(mesh):
    placed = (P("frame", "pack", None), P(), P("frame", "pack"), P("frame", "pack", None))
    return jax.shard_map(
        per_device,
        mesh=mesh,
        in_specs=placed,
        out_specs=(P("frame", "pack", None), P("frame", "pack", None)),
        check_vma=False,
    )
```

profile of v0, /device:TPU:1, one launch (start us, length us, event | category | flops | bytes accessed | tf_op | source)
XLA Modules:
  0.0 583.3 jit_solution(14545785212371072562)
XLA Ops:
  8.8 13.4 %fusion.9 = bf16[512,3360]{0,1:T(8,128)(2,1)} fusion(bf16[2240,3360]{1,0:T(8,128)(2,1)} %param.9, bf16[1,512,2240]{1,2,0:T(8,128)(2,1)S(1)} %copy-done), kind=kOutput, calls=%fused_computation.30 | convolution fusion | flops 7707033600 | bytes 20787200 | tf_op jit(solution)/shard_map/dot_general | solution.py:98
  28.2 5.7 copy.41
  33.8 10.4 %scatter_custom_fusion = bf16[768,3360]{1,0:T(8,128)(2,1)} fusion(s32[512]{0:T(512)S(1)} %bitcast.117, bf16[512,3360]{1,0:T(8,128)(2,1)} %copy.41, bf16[]{:T(256)} %constant.68.clone.1), kind=kCustom, calls=%fused_computation.27 | custom fusion | bytes 5161472 | tf_op jit(solution)/shard_map/scatter | solution.py:110
  44.3 16.6 %reshape.106 = bf16[2,384,3,10,112]{4,3,2,1,0:T(8,128)(2,1)} reshape(bf16[768,3360]{1,0:T(8,128)(2,1)} %scatter_custom_fusion) | data formatting | bytes 10321920 | tf_op jit(solution)/shard_map/reshape;reshape | solution.py:37
  60.9 6.7 %fusion.32 = (bf16[2,384,1,10,112]{4,3,2,1,0:T(8,128)(2,1)}, bf16[2,384,1,10,112]{4,3,2,1,0:T(8,128)(2,1)}, bf16[2,384,1,10,112]{4,3,2,1,0:T(8,128)(2,1)}) fusion(bf16[2,384,3,10,112]{4,3,2,1,0:T(8,128)(2,1)} %reshape.106), kind=kLoop, calls=%fused_computation.64 | loop fusion | bytes 10321920 | tf_op jit(solution)/shard_map/slice | solution.py:52
  67.5 5.0 copy.65
  72.5 5.4 copy.66
  81.2 64.3 %all-reduce.3.cloned.1.call-done = f32[2,10,112,112]{3,2,1,0:T(8,128)} async-done(((f32[2,10,112,112]{3,2,1,0:T(8,128)}), f32[2,10,112,112]{3,2,1,0:T(8,128)}) %all-reduce.3.cloned.1.call-update) | async-done | bytes 1003536 | tf_op jit(solution)/shard_map/psum | solution.py:120
  145.6 4.7 copy.67
  159.7 4.9 reshape.67
  165.1 24.4 %psum.29 = f32[2,10,112]{2,1,0:T(8,128)S(1)} all-reduce(f32[2,10,112]{2,1,0:T(8,128)S(1)} %convert_reduce_fusion), channel_id=1, replica_groups=mesh['frame'=16,'pack'=8] {'pack'}, use_global_device_ids=true, to_apply=%region_6.7 | all-reduce | flops 2240 | bytes 17920 | tf_op jit(solution)/shard_map/psum | solution.py:120
  189.4 21.1 %all-gather.1 = f32[32,10,112]{2,1,0:T(8,128)S(1)} all-gather(f32[2,10,112]{2,1,0:T(8,128)S(1)} %psum.29), channel_id=3, replica_groups=mesh['frame'=16,'pack'=8] {'frame'}, dimensions={0}, use_global_device_ids=true | all-gather | bytes 152320 | tf_op jit(solution)/shard_map/all_gather | solution.py:18
  210.5 58.9 %all-gather.7.cloned.1.call-done = f32[32,10,112,112]{3,2,1,0:T(8,128)} async-done(((f32[2,10,112,112]{3,2,1,0:T(8,128)}), f32[32,10,112,112]{3,2,1,0:T(8,128)}) %all-gather.7.cloned.1.call-update) | async-done | bytes 16056336 | tf_op jit(solution)/shard_map/all_gather | solution.py:18
  276.2 83.4 %all-reduce.5.cloned.1.call-done = f32[2,10,112,112]{3,2,1,0:T(8,128)} async-done(((f32[2,10,112,112]{3,2,1,0:T(8,128)}), f32[2,10,112,112]{3,2,1,0:T(8,128)}) %all-reduce.5.cloned.1.call-update) | async-done | bytes 1003536 | tf_op jit(solution)/shard_map/psum | solution.py:133
  363.9 4.7 copy.59
  368.6 4.7 reshape.104
  378.1 24.8 %psum.31 = f32[2,10,112]{2,1,0:T(8,128)S(1)} all-reduce(f32[2,10,112]{2,1,0:T(8,128)S(1)} %fusion.3), channel_id=1, replica_groups=mesh['frame'=16,'pack'=8] {'pack'}, use_global_device_ids=true, to_apply=%region_14.15 | all-reduce | flops 2240 | bytes 17920 | tf_op jit(solution)/shard_map/psum | solution.py:133
  402.9 22.0 %all-gather.3 = f32[32,10,112]{2,1,0:T(8,128)} all-gather(f32[2,10,112]{2,1,0:T(8,128)S(1)} %psum.31), channel_id=5, replica_groups=mesh['frame'=16,'pack'=8] {'frame'}, dimensions={0}, use_global_device_ids=true | all-gather | bytes 152320 | tf_op jit(solution)/shard_map/all_gather | solution.py:18
  429.0 54.4 %all-gather.9.cloned.1.call-done = f32[32,10,112,112]{3,2,1,0:T(8,128)} async-done(((f32[2,10,112,112]{3,2,1,0:T(8,128)}), f32[32,10,112,112]{3,2,1,0:T(8,128)}) %all-gather.9.cloned.1.call-update) | async-done | bytes 16056336 | tf_op jit(solution)/shard_map/all_gather | solution.py:18
  483.5 34.1 %while.27 = (s32[]{:T(128)}, f32[2,10,112,112]{3,2,1,0:T(8,128)S(1)}, f32[2,10,112]{2,1,0:T(8,128)S(1)}, s32[]{:T(128)}, f32[16,2,10,112,112]{4,3,2,1,0:T(8,128)...) while((s32[]{:T(128)}, f32[2,10,112,112]{3,2,1,0:T(8,128)S(1)}, ...), condition=%wide.region_16.17_spmd, body=%wide.region_15.16_spmd.sunk | while | flops 253126 | bytes 3037595 | solution.py:27
  525.0 13.0 %copy.60 = bf16[2,384,3,10,112]{4,3,2,1,0:T(8,128)(2,1)} copy(bf16[2,384,3,10,112]{1,4,3,0,2:T(8,128)(2,1)} %pad_maximum_fusion) | data formatting | bytes 10321920 | tf_op jit(solution)/shard_map/convert_element_type | solution.py:90
  538.0 13.7 %reshape.105 = bf16[768,3360]{1,0:T(8,128)(2,1)} reshape(bf16[2,384,3,10,112]{4,3,2,1,0:T(8,128)(2,1)} %copy.60) | data formatting | bytes 10321920 | tf_op jit(solution)/shard_map/convert_element_type | solution.py:90
  551.6 10.9 %gather_fusion.1 = bf16[512,3360]{1,0:T(8,128)(2,1)} fusion(bf16[768,3360]{1,0:T(8,128)(2,1)} %reshape.105, s32[1024]{0:T(1024)S(1)} %pad_clamp_fusion), kind=kCustom, calls=%fused_computation.1 | custom fusion | bytes 6883328 | tf_op jit(solution)/shard_map/gather | solution.py:147
  562.5 14.1 %fusion.1 = bf16[1,512,2240]{1,2,0:T(8,128)(2,1)} fusion(bf16[512,3360]{1,0:T(8,128)(2,1)} %gather_fusion.1, bf16[2240,3360]{1,0:T(8,128)(2,1)} %param.9), kind=kOutput, calls=%fused_computation.14 | convolution fusion | flops 7708180480 | bytes 20787200 | tf_op jit(solution)/shard_map/tk,dk->td/dot_general | solution.py:148
  (102 shorter events, 81.9 us)
Async XLA Ops:
  7.2 1.7 copy-start
  7.2 138.3 %all-reduce.3.cloned.1.call-start = ((), (), s32[]{:S(2)}) async-start(), calls=%async_computation | async-start | bytes 2293760 | tf_op jit(solution)/shard_map/psum | solution.py:120
  24.3 0.7 copy-start.12
  24.3 1.8 slice-start
  72.5 92.1 %copy-start.2 = (bf16[2,384,1,10,112]{1,4,3,0,2:T(8,128)(2,1)}, bf16[2,384,1,10,112]{1,4,3,0,2:T(8,128)(2,1)S(1)}, u32[]{:S(2)}) copy-start(bf16[2,384,1,10,112]{1,4,3,0,2:T(8,128)(2,1)S(1)} %copy.65) | copy-start | bytes 5160964
  81.1 188.3 %all-gather.7.cloned.1.call-start = ((), (), s32[]{:S(2)}) async-start(), calls=%async_computation.2 | async-start | bytes 19496960 | tf_op jit(solution)/shard_map/all_gather | solution.py:18
  145.5 214.1 %all-reduce.5.cloned.1.call-start = ((), (), s32[]{:S(2)}) async-start(), calls=%async_computation.1 | async-start | bytes 2293760 | tf_op jit(solution)/shard_map/psum | solution.py:133
  271.8 87.9 %copy-start.11 = (f32[2,384,10]{1,2,0:T(8,128)}, f32[2,384,10]{1,2,0:T(8,128)S(1)}, u32[]{:S(2)}) copy-start(f32[2,384,10]{1,2,0:T(8,128)S(1)} %broadcast_add_fusion) | copy-start | bytes 92164
  276.1 83.5 %copy-start.6 = (f32[2,10,112,112]{3,2,1,0:T(8,128)S(1)}, f32[2,10,112,112]{3,2,1,0:T(8,128)}, u32[]{:S(2)}) copy-start(f32[2,10,112,112]{3,2,1,0:T(8,128)} %all-reduce.3.cloned.1.call-done) | copy-start | bytes 3010564
  276.2 207.3 %all-gather.9.cloned.1.call-start = ((), (), s32[]{:S(2)}) async-start(), calls=%async_computation.3 | async-start | bytes 19496960 | tf_op jit(solution)/shard_map/all_gather | solution.py:18
  359.8 4.1 copy-start.9
  375.4 2.2 copy-start.5
  375.4 49.5 %copy-start.10 = (bf16[2,10,112,112]{3,2,1,0:T(8,128)(2,1)S(1)}, bf16[2,10,112,112]{3,2,1,0:T(8,128)(2,1)}, u32[]{:S(2)}) copy-start(bf16[2,10,112,112]{3,2,1,0:T(8,128)(2,1)} %copy-done.9) | copy-start | bytes 1505284
  483.5 34.1 %copy-start.7 = (f32[2,10,112,112]{3,2,1,0:T(8,128)S(1)}, f32[2,10,112,112]{3,2,1,0:T(8,128)}, u32[]{:S(2)}) copy-start(f32[2,10,112,112]{3,2,1,0:T(8,128)} %all-reduce.5.cloned.1.call-done) | copy-start | bytes 3010564
  517.6 1.5 copy-start.3
  519.0 1.5 copy-start.4
  520.5 1.5 copy-start.8
  562.5 14.1 %copy-start.1 = (bf16[1,512,2240]{1,2,0:T(8,128)(2,1)S(1)}, bf16[1,512,2240]{1,2,0:T(8,128)(2,1)}, u32[]{:S(2)}) copy-start(bf16[1,512,2240]{1,2,0:T(8,128)(2,1)} %param.8) | copy-start | bytes 6881284
Sparse Core Ops, SparseCore 0:
  81.2 64.1 all-reduce.2
  147.7 121.7 all-gather.6
  276.3 83.2 all-reduce.4
  361.7 121.7 all-gather.8
where the time goes:
time: 595 us; the launch traced here: 583 us
  waiting for transfers between devices  261 us (44%)
  local copies, waits for them, and re-layouts  125 us (21%)
  blocking collectives  92.3 us (16%)
  other arithmetic  45.8 us (8%)
  matrix products  44.7 us (8%)
  between operations  14.3 us (2%)
    all_gather x2, waiting for transfers between devices, carried_in(): gathered = jax.tree.map(lambda a: lax.all_gather(a, axis), part)  113 us
    psum x1, waiting for transfers between devices, per_device(): grad_block, dnorm_block = lax.psum((local_grad, local_dnorm), 'pack')  83.4 us
    psum x1, waiting for transfers between devices, per_device(): block_state, block_norm = lax.psum((local_state, local_norm), 'pack')  64.3 us
    all_gather x2, blocking collectives, carried_in(): gathered = jax.tree.map(lambda a: lax.all_gather(a, axis), part)  43.1 us
    add x30, other arithmetic, add_pair(): return (earlier[0] + later[0], earlier[1] + later[1])  33.8 us
    convert_element_type x2, local copies, waits for them, and re-layouts, back_terms(): jnp.stack([query_grad, key_grad, value_grad], axis=2).astype(jnp.bfloat16)  26.6 us
    psum x1, blocking collectives, per_device(): grad_block, dnorm_block = lax.psum((local_grad, local_dnorm), 'pack')  24.8 us
    psum x1, blocking collectives, per_device(): block_state, block_norm = lax.psum((local_state, local_norm), 'pack')  24.4 us
  transfers between devices with their start and end apart: 4, of which 4 were waited for; matrix products, arithmetic and copies ran while one was open for 7% of the time, Pallas kernels for 0%

commit v1 on v0

v1 whole, which is shorter than its diff:
```python
import jax
import jax.numpy as jnp
from jax import lax
from jax.experimental import pallas as pl
from jax.experimental.pallas import tpu as pltpu
from jax.sharding import PartitionSpec as P

F32 = jnp.float32
BF16 = jnp.bfloat16
MESH = pl.DeviceIdType.MESH
EPS = 1e-06
HEAD = 112
HEADS = 10
WIDE = 128
TOK = 512
D = 2240
HD = HEADS * HEAD
COLS = 3 * HD
FLAT = HEADS * WIDE
RING = 4
QUARTER = FLAT // RING
NROWS = 24


def tn(a, b):
    return lax.dot_general(a, b, (((0,), (0,)), ((), ())), preferred_element_type=F32)


def nt(a, b):
    return lax.dot_general(a, b, (((1,), (1,)), ((), ())), preferred_element_type=F32)


def nn(a, b):
    return lax.dot_general(a, b, (((1,), (0,)), ((), ())), preferred_element_type=F32)


def lanes(shape):
    return lax.broadcasted_iota(jnp.int32, shape, len(shape) - 1)


class Place:
    def __init__(self):
        frame = lax.axis_index("frame")
        pack = lax.axis_index("pack")
        self.x, self.y = frame // RING, frame % RING
        self.z, self.c = pack // 2, pack % 2
        self.frame, self.pack = frame, pack

    def core(self):
        return {"frame": self.frame, "pack": self.z * 2 + (1 - self.c)}

    def along_z(self, j):
        return {"frame": self.frame, "pack": ((self.z + j) % RING) * 2 + self.c}

    def along_y(self, j):
        return {"frame": self.x * RING + (self.y + j) % RING, "pack": self.pack}

    def along_x(self, j):
        return {"frame": ((self.x + j) % RING) * RING + self.y, "pack": self.pack}

    def peers(self):
        out = [self.core()]
        for j in (1, 2, 3):
            out += [self.along_z(j), self.along_y(j), self.along_x(j)]
        return out

    def earlier(self, at, j, reverse):
        return (j > at) if reverse else (j <= at)


class Links:
    def __init__(self, send, recv):
        self.send, self.recv, self.at, self.copies = send, recv, 0, []

    def start(self, src, dst, device):
        copy = pltpu.make_async_remote_copy(
            src_ref=src,
            dst_ref=dst,
            send_sem=self.send.at[self.at],
            recv_sem=self.recv.at[self.at],
            device_id=device,
            device_id_type=MESH,
        )
        self.at += 1
        copy.start()
        self.copies.append(copy)
        return copy

    def drain(self):
        for copy in self.copies:
            copy.wait_send()


class Small:
    def __init__(self, place, links, refs, reverse):
        self.p, self.l, self.reverse = place, links, reverse
        self.own, self.rc, self.sz, self.rz, self.sy, self.ry, self.sx, self.rx, self.inc, self.out = refs

    def s0(self):
        self.w = [self.l.start(self.own, self.rc, self.p.core())]

    def wait(self):
        for w in self.w:
            w.wait_recv()

    def s1(self):
        self.wait()
        self.sz[...] = self.own[...] + self.rc[...]
        self.w = [self.l.start(self.sz, self.rz.at[j - 1], self.p.along_z(j)) for j in (1, 2, 3)]

    def s2(self):
        self.wait()
        self.sy[...] = self.sz[...] + self.rz[0] + self.rz[1] + self.rz[2]
        self.w = [self.l.start(self.sy, self.ry.at[j - 1], self.p.along_y(j)) for j in (1, 2, 3)]

    def s3(self):
        self.wait()
        total = self.sy[...]
        part = total
        for j in (1, 2, 3):
            term = self.ry[j - 1]
            total = total + term
            part = part + jnp.where(self.p.earlier(self.p.y, j, self.reverse), term, 0.0)
        self.sx[...] = total
        self.inc[...] = part
        self.w = [self.l.start(self.sx, self.rx.at[j - 1], self.p.along_x(j)) for j in (1, 2, 3)]

    def s4(self):
        self.wait()
        part = self.inc[...]
        for j in (1, 2, 3):
            part = part + jnp.where(self.p.earlier(self.p.x, j, self.reverse), self.rx[j - 1], 0.0)
        self.out[...] = part.astype(BF16).astype(F32)


class Big:
    def __init__(self, place, links, refs, reverse):
        self.p, self.l, self.reverse = place, links, reverse
        self.acc, self.sc, self.rc, self.sz, self.rz, self.sy, self.ry, self.sx, self.rx, self.inc, self.out = refs

    def put(self, rows, both):
        own, other = both[:, :WIDE], both[:, WIDE:]
        first = self.p.c == 0
        self.acc[rows, :] = jnp.where(first, own, other)
        self.sc[rows, :] = jnp.where(first, other, own).astype(BF16)

    def wait(self):
        for w in self.w:
            w.wait_recv()

    def s0(self):
        self.w = [self.l.start(self.sc, self.rc, self.p.core())]

    def s1(self):
        self.wait()
        for q in range(RING):
            rows = slice(q * QUARTER, (q + 1) * QUARTER)
            total = self.acc[rows, :] + self.rc[rows, :].astype(F32)
            self.acc[rows, :] = total
            self.sz[q] = total.astype(BF16)
        self.w = [
            self.l.start(self.sz.at[(self.p.z + j) % RING], self.rz.at[j - 1], self.p.along_z(j))
            for j in (1, 2, 3)
        ]

    def s2(self):
        self.wait()
        mine = self.acc[pl.ds(pl.multiple_of(self.p.z * QUARTER, 64), QUARTER), :]
        total = mine + self.rz[0].astype(F32) + self.rz[1].astype(F32) + self.rz[2].astype(F32)
        self.inc[...] = total
        self.sy[...] = total.astype(BF16)
        self.w = [self.l.start(self.sy, self.ry.at[j - 1], self.p.along_y(j)) for j in (1, 2, 3)]

    def s3(self):
        self.wait()
        total = self.inc[...]
        part = total
        for j in (1, 2, 3):
            term = self.ry[j - 1].astype(F32)
            total = total + term
            part = part + jnp.where(self.p.earlier(self.p.y, j, self.reverse), term, 0.0)
        self.inc[...] = part
        self.sx[...] = total.astype(BF16)
        self.w = [self.l.start(self.sx, self.rx.at[j - 1], self.p.along_x(j)) for j in (1, 2, 3)]

    def piece(self, clip, quarter):
        return self.out.at[clip, pl.ds(pl.multiple_of(quarter * QUARTER, 64), QUARTER), :]

    def s4(self):
        self.wait()
        part = self.inc[...]
        for j in (1, 2, 3):
            part = part + jnp.where(
                self.p.earlier(self.p.x, j, self.reverse), self.rx[j - 1].astype(F32), 0.0
            )
        here = self.piece(self.p.c, self.p.z)
        here[...] = part.astype(BF16)
        self.w = [self.l.start(here, here, self.p.along_z(j)) for j in (1, 2, 3)]
        self.wc = [self.l.start(here, here, self.p.core())]

    def s5(self):
        for j in (1, 2, 3):
            self.w[j - 1].wait_recv()
            here = self.piece(self.p.c, (self.p.z - j + RING) % RING)
            self.wc.append(self.l.start(here, here, self.p.core()))

    def s6(self):
        for w in self.wc:
            w.wait_recv()


def small_scratch():
    one = pltpu.VMEM((NROWS, WIDE), F32)
    three = pltpu.VMEM((3, NROWS, WIDE), F32)
    return [one, one, one, three, one, three, one, three, one, one]


def big_scratch():
    three = pltpu.VMEM((3, QUARTER, WIDE), BF16)
    one = pltpu.VMEM((QUARTER, WIDE), BF16)
    return [
        pltpu.VMEM((FLAT, WIDE), F32),
        pltpu.VMEM((FLAT, WIDE), BF16),
        pltpu.VMEM((FLAT, WIDE), BF16),
        pltpu.VMEM((RING, QUARTER, WIDE), BF16),
        three,
        one,
        three,
        one,
        three,
        pltpu.VMEM((QUARTER, WIDE), F32),
        pltpu.VMEM((2, FLAT, WIDE), BF16),
    ]


COPIES = 2 * 10 + 2 * 17
SPANS = ((1024, 2304), (2304, COLS), (0, 1024))


def kernel(
    x_hbm, w_hbm, clip_hbm, og_hbm, att_hbm, ig_hbm,
    xv, wv, clipv, ogv, proj, feat, og, ng, inv, m0, m1, dg, grads, acc, outv, attp, attv,
    lsem, send, recv, *rest,
):
    ns, ds_, bs, bg = rest[:10], rest[10:20], rest[20:31], rest[31:42]
    p = Place()
    barrier = pltpu.get_barrier_semaphore()
    peers = p.peers()
    for peer in peers:
        pl.semaphore_signal(barrier, inc=1, device_id=peer, device_id_type=MESH)

    loads = [
        pltpu.make_async_copy(clip_hbm, clipv, lsem.at[0]),
        pltpu.make_async_copy(x_hbm.at[0], xv, lsem.at[1]),
    ]
    for i, (lo, hi) in enumerate(SPANS):
        loads.append(
            pltpu.make_async_copy(w_hbm.at[:, lo:hi], wv.at[:, lo:hi], lsem.at[2 + i])
        )
    loads.append(pltpu.make_async_copy(og_hbm.at[0], ogv, lsem.at[5]))
    for i in (0, 1, 2, 5, 3, 4):
        loads[i].start()

    links = Links(send, recv)
    norm = Small(p, links, ns, False)
    dnorm = Small(p, links, ds_, True)
    state = Big(p, links, bs, False)
    grad = Big(p, links, bg, True)

    def clip_masks():
        loads[0].wait()
        row = clipv[...].astype(F32)
        for t in range(TOK // WIDE):
            tile = jnp.broadcast_to(row[:, t * WIDE : (t + 1) * WIDE], (WIDE, WIDE)).T
            rows = slice(t * WIDE, (t + 1) * WIDE)
            m1[rows, :] = tile.astype(BF16)
            m0[rows, :] = (1.0 - tile).astype(BF16)

    def project(start, count):
        def one(t, carry):
            c0 = pl.multiple_of(start + t * 256, WIDE)
            r = nn(xv[...], wv[:, pl.ds(c0, 256)])
            relu = c0 + lanes(r.shape) < 2 * HD
            proj[:, pl.ds(c0, 256)] = jnp.where(relu, jnp.maximum(r, 0.0), r).astype(BF16)
            return carry

        lax.fori_loop(0, count, one, 0)

    def project_tail():
        proj[:, 3328:COLS] = nn(xv[...], wv[:, 3328:COLS]).astype(BF16)

    def expand(src, width, head, dst, at):
        tile, off = (HEAD * head) // WIDE, (HEAD * head) % WIDE
        lo = src[:, tile * WIDE : min((tile + 1) * WIDE, width)]
        lane = lanes((TOK, WIDE))
        if off > WIDE - HEAD:
            hi = src[:, (tile + 1) * WIDE : min((tile + 2) * WIDE, width)].astype(F32)
            if hi.shape[1] < WIDE:
                hi = jnp.concatenate([hi, jnp.zeros((TOK, WIDE - hi.shape[1]), F32)], axis=1)
            lo = jnp.where(lane >= off, lo.astype(F32), hi)
        else:
            lo = lo.astype(F32)
        if off:
            lo = pltpu.roll(lo, WIDE - off, 1)
        dst[at] = jnp.where(lane < HEAD, lo, 0.0).astype(BF16)

    def expand_feat(lo, hi):
        for head in range(lo, hi):
            expand(proj, 3456, head, feat, head)

    def masked(v):
        return jnp.concatenate([v * m0[...], v * m1[...]], axis=1)

    def rows_of(h):
        return pl.ds(pl.multiple_of(h * WIDE, WIDE), WIDE)

    def clip_sums(ref, h, v):
        ref[pl.ds(h, 1), :] = jnp.sum(v * m0[...].astype(F32), axis=0, keepdims=True)
        ref[pl.ds(HEADS + h, 1), :] = jnp.sum(v * m1[...].astype(F32), axis=0, keepdims=True)

    def norm_local():
        norm.own[...] = jnp.zeros_like(norm.own)

        def one(h, carry):
            clip_sums(norm.own, h, feat[HEADS + h].astype(F32))
            return carry

        lax.fori_loop(0, HEADS, one, 0)

    def state_local():
        def one(h, carry):
            state.put(rows_of(h), tn(feat[HEADS + h], masked(feat[2 * HEADS + h])))
            return carry

        lax.fori_loop(0, HEADS, one, 0)

    def grad_local():
        def one(h, carry):
            q = feat[h]
            n0 = norm.out[pl.ds(h, 1), :].astype(BF16)
            n1 = norm.out[pl.ds(HEADS + h, 1), :].astype(BF16)
            side = jnp.concatenate(
                [jnp.broadcast_to(n0, (WIDE, WIDE)), jnp.broadcast_to(n1, (WIDE, WIDE))], axis=1
            )
            r = 1.0 / (nt(masked(q), side) + EPS)
            inv[h] = r
            g = (og[h].astype(F32) * r).astype(BF16)
            ng[h] = g
            grad.put(rows_of(h), tn(q, masked(g)))
            return carry

        lax.fori_loop(0, HEADS, one, 0)

    def attend():
        dnorm.own[...] = jnp.zeros_like(dnorm.own)

        def one(h, carry):
            q = feat[h]
            s0, s1 = state.out[0, rows_of(h), :], state.out[1, rows_of(h), :]
            r = inv[h]
            att = nn(masked(q), jnp.concatenate([s0, s1], axis=0)) * r
            attp[h] = att.astype(BF16)
            d = -jnp.sum(og[h].astype(F32) * att, axis=1, keepdims=True) * r
            q32 = q.astype(F32)
            clip_sums(dnorm.own, h, q32 * d)
            n0, n1 = norm.out[pl.ds(h, 1), :], norm.out[pl.ds(HEADS + h, 1), :]
            qg = nt(masked(ng[h]), jnp.concatenate([s0, s1], axis=1))
            qg = qg + d * jnp.where(m1[...].astype(F32) > 0, n1, n0)
            dg[h] = jnp.where(q32 > 0, qg, 0.0).astype(BF16)
            return carry

        lax.fori_loop(0, HEADS, one, 0)

    def value_grads():
        def one(h, carry):
            g0, g1 = grad.out[0, rows_of(h), :], grad.out[1, rows_of(h), :]
            k = feat[HEADS + h]
            dg[2 * HEADS + h] = nn(masked(k), jnp.concatenate([g0, g1], axis=0)).astype(BF16)
            return carry

        lax.fori_loop(0, HEADS, one, 0)

    def key_grads():
        def one(h, carry):
            g0, g1 = grad.out[0, rows_of(h), :], grad.out[1, rows_of(h), :]
            kg = nt(masked(feat[2 * HEADS + h]), jnp.concatenate([g0, g1], axis=1))
            d0, d1 = dnorm.out[pl.ds(h, 1), :], dnorm.out[pl.ds(HEADS + h, 1), :]
            kg = kg + jnp.where(m1[...].astype(F32) > 0, d1, d0)
            keep = feat[HEADS + h].astype(F32) > 0
            dg[HEADS + h] = jnp.where(keep, kg, 0.0).astype(BF16)
            return carry

        lax.fori_loop(0, HEADS, one, 0)

    def flat_tile(src, tile):
        head, off = (WIDE * tile) // HEAD, (WIDE * tile) % HEAD
        count = HEAD - off
        a = src[head].astype(F32)
        if off:
            a = pltpu.roll(a, WIDE - off, 1)
        if head + 1 < src.shape[0]:
            b = pltpu.roll(src[head + 1].astype(F32), count, 1)
            a = jnp.where(lanes(a.shape) < count, a, b)
        return a.astype(BF16)

    def flatten_grads(lo, hi):
        for tile in range(lo, hi):
            width = min(WIDE, COLS - tile * WIDE)
            grads[:, tile * WIDE : tile * WIDE + width] = flat_tile(dg, tile)[:, :width]

    def back(lo, hi, kind):
        def step(n0, count):
            r = nt(grads[:, lo:hi], wv[pl.ds(n0, count), lo:hi])
            at = (slice(None), pl.ds(n0, count))
            if kind > 0:
                r = r + acc[at]
            if kind < 2:
                acc[at] = r
            else:
                outv[at] = r.astype(BF16)

        def one(t, carry):
            step(pl.multiple_of(t * 256, 256), 256)
            return carry

        lax.fori_loop(0, D // 256, one, 0)
        step((D // 256) * 256, D % 256)

    clip_masks()
    loads[1].wait()
    loads[2].wait()
    project(1024, 5)
    expand_feat(HEADS, 2 * HEADS)
    norm_local()
    pl.semaphore_wait(barrier, len(peers))
    norm.s0()
    loads[3].wait()
    project(2304, 1)
    norm.s1()
    project(2560, 3)
    project_tail()
    norm.s2()
    expand_feat(2 * HEADS, 3 * HEADS)
    state_local()
    state.s0()
    norm.s3()
    loads[4].wait()
    project(0, 1)
    state.s1()
    project(256, 3)
    norm.s4()
    state.s2()
    expand_feat(0, HEADS)
    loads[5].wait()
    for head in range(HEADS):
        expand(ogv, HD, head, og, head)
    grad_local()
    grad.s0()
    state.s3()
    grad.s1()
    state.s4()
    grad.s2()
    state.s5()
    grad.s3()
    state.s6()
    attend()
    dnorm.s0()
    grad.s4()
    flatten_grads(0, 8)
    for tile in range(9):
        width = min(WIDE, HD - tile * WIDE)
        attv[:, tile * WIDE : tile * WIDE + width] = flat_tile(attp, tile)[:, :width]
    stores = [pltpu.make_async_copy(attv, att_hbm.at[0], lsem.at[0])]
    stores[0].start()
    dnorm.s1()
    grad.s5()
    back(0, 1024, 0)
    dnorm.s2()
    grad.s6()
    value_grads()
    dnorm.s3()
    flatten_grads(18, 27)
    back(2304, COLS, 1)
    dnorm.s4()
    key_grads()
    flatten_grads(8, 18)
    back(1024, 2304, 2)
    stores.append(pltpu.make_async_copy(outv, ig_hbm.at[0], lsem.at[1]))
    stores[1].start()
    links.drain()
    for store in stores:
        store.wait()


def per_device(inputs, weight, clip_of_row, out_grad):
    anywhere = pl.BlockSpec(memory_space=pl.ANY)
    heads = lambda n, t: pltpu.VMEM((n, TOK, WIDE), t)
    return pl.pallas_call(
        kernel,
        out_shape=(
            jax.ShapeDtypeStruct((1, TOK, HD), BF16),
            jax.ShapeDtypeStruct((1, TOK, D), BF16),
        ),
        in_specs=[anywhere] * 4,
        out_specs=(anywhere, anywhere),
        scratch_shapes=[
            pltpu.VMEM((TOK, D), BF16),
            pltpu.VMEM((D, COLS), BF16),
            pltpu.VMEM((1, TOK), jnp.int32),
            pltpu.VMEM((TOK, HD), BF16),
            pltpu.VMEM((TOK, 3456), BF16),
            heads(3 * HEADS, BF16),
            heads(HEADS, BF16),
            heads(HEADS, BF16),
            heads(HEADS, F32),
            pltpu.VMEM((TOK, WIDE), BF16),
            pltpu.VMEM((TOK, WIDE), BF16),
            heads(3 * HEADS, BF16),
            pltpu.VMEM((TOK, COLS), BF16),
            pltpu.VMEM((TOK, D), F32),
            pltpu.VMEM((TOK, D), BF16),
            heads(HEADS, BF16),
            pltpu.VMEM((TOK, HD), BF16),
            pltpu.SemaphoreType.DMA((6,)),
            pltpu.SemaphoreType.DMA((COPIES,)),
            pltpu.SemaphoreType.DMA((COPIES,)),
            *small_scratch(),
            *small_scratch(),
            *big_scratch(),
            *big_scratch(),
        ],
        compiler_params=pltpu.CompilerParams(
            collective_id=0, has_side_effects=True, vmem_limit_bytes=67000000
        ),
    )(inputs, weight, clip_of_row, out_grad)


def solution(mesh):
    placed = (P("frame", "pack", None), P(), P("frame", "pack"), P("frame", "pack", None))
    return jax.shard_map(
        per_device,
        mesh=mesh,
        in_specs=placed,
        out_specs=(P("frame", "pack", None), P("frame", "pack", None)),
        check_vma=False,
    )
```

time: 595 us -> 94.7 us (0.16)
  the two profiles are of different devices: /device:TPU:1 before, /device:TPU:0 now
where the time goes in v1:
time: 94.7 us; the launch traced here: 94.5 us
  Pallas kernels  82.2 us (87%)
  local copies, waits for them, and re-layouts  11.7 us (12%)
    pallas_call x1, Pallas kernels, per_device(): pl.pallas_call(kernel, out_shape=(jax.ShapeDtypeStruct((1, TOK, HD), BF16...  82.2 us
    pallas_call x2, local copies, waits for them, and re-layouts, per_device(): pl.pallas_call(kernel, out_shape=(jax.ShapeDtypeStruct((1, TOK, HD), BF16...  6.61 us
    unnamed x4, local copies, waits for them, and re-layouts  5.07 us

profile of v1, /device:TPU:0, one launch (start us, length us, event | category | flops | bytes accessed | tf_op | source)
XLA Modules:
  0.0 94.5 jit_solution(7483423787558840741)
XLA Ops:
  0.6 0.0 copy-start
  0.6 2.5 %copy.7.og_hbm = bf16[1,512,1120]{2,1,0:T(8,128)(2,1)} copy(bf16[1,512,1120]{1,2,0:T(8,128)(2,1)} %param.7) | data formatting | bytes 2293760 | tf_op args[3]
  3.2 0.0 copy-done
  3.2 2.5 %copy.6.x_hbm = bf16[1,512,2240]{2,1,0:T(8,128)(2,1)} copy(bf16[1,512,2240]{1,2,0:T(8,128)(2,1)S(1)} %copy-done) | data formatting | bytes 4587520 | tf_op args[0]
  5.7 82.2 %shard_map.59 = (bf16[1,512,1120]{2,1,0:T(8,128)(2,1)}, bf16[1,512,2240]{2,1,0:T(8,128)(2,1)}) custom-call(bf16[1,512,2240]{2,1,0:T(8,128)(2,1)} %copy.6.x_hbm, bf16[2240,3360]{1,0:T(8,128)(2,1)} %w_hbm.1, s32[1,512]{1,0:T(1,128)} %clip_hbm.1, bf16[1,512,1120]{2,1,0:T(8,128)(2,1)} %copy.7.og_hbm), custom_call_target="tpu_custom_call" | custom-call | tf_op jit(solution)/shard_map/pallas_call | solution.py:498
  87.9 2.4 %copy.8 = bf16[1,512,1120]{1,2,0:T(8,128)(2,1)} copy(bf16[1,512,1120]{2,1,0:T(8,128)(2,1)} %get-tuple-element.2) | data formatting | bytes 2293760 | tf_op jit(solution)/shard_map/pallas_call | solution.py:498
  90.3 4.3 %copy.9 = bf16[1,512,2240]{1,2,0:T(8,128)(2,1)} copy(bf16[1,512,2240]{2,1,0:T(8,128)(2,1)} %get-tuple-element.3) | data formatting | bytes 4587520 | tf_op jit(solution)/shard_map/pallas_call | solution.py:498
Async XLA Ops:
  0.6 2.5 %copy-start = (bf16[1,512,2240]{1,2,0:T(8,128)(2,1)S(1)}, bf16[1,512,2240]{1,2,0:T(8,128)(2,1)}, u32[]{:S(2)}) copy-start(bf16[1,512,2240]{1,2,0:T(8,128)(2,1)} %param.4) | copy-start | bytes 6881284

commit v2 on v1

v2 whole, which is shorter than its diff:
```python
import jax
import jax.numpy as jnp
from jax import lax
from jax.experimental import pallas as pl
from jax.experimental.pallas import tpu as pltpu
from jax.sharding import PartitionSpec as P

F32 = jnp.float32
BF16 = jnp.bfloat16
MESH = pl.DeviceIdType.MESH
EPS = 1e-06
HEAD = 112
HEADS = 10
WIDE = 128
TOK = 512
D = 2240
HD = HEADS * HEAD
COLS = 3 * HD
RING = 4
GROUPS = 2
PER = HEADS // GROUPS
ROWS = 576
QUARTER = ROWS // RING
NROWS = 24
TILES = 9


def tn(a, b):
    return lax.dot_general(a, b, (((0,), (0,)), ((), ())), preferred_element_type=F32)


def nt(a, b):
    return lax.dot_general(a, b, (((1,), (1,)), ((), ())), preferred_element_type=F32)


def nn(a, b):
    return lax.dot_general(a, b, (((1,), (0,)), ((), ())), preferred_element_type=F32)


class Place:
    def __init__(self):
        frame = lax.axis_index("frame")
        pack = lax.axis_index("pack")
        self.x, self.y = frame // RING, frame % RING
        self.z, self.c = pack // 2, pack % 2
        self.frame, self.pack = frame, pack

    def core(self):
        return {"frame": self.frame, "pack": self.z * 2 + (1 - self.c)}

    def along_z(self, j):
        return {"frame": self.frame, "pack": ((self.z + j) % RING) * 2 + self.c}

    def along_y(self, j):
        return {"frame": self.x * RING + (self.y + j) % RING, "pack": self.pack}

    def along_x(self, j):
        return {"frame": ((self.x + j) % RING) * RING + self.y, "pack": self.pack}

    def peers(self):
        out = [self.core()]
        for j in (1, 2, 3):
            out += [self.along_z(j), self.along_y(j), self.along_x(j)]
        return out

    def earlier(self, at, j, reverse):
        return (j > at) if reverse else (j <= at)


class Links:
    def __init__(self, send, recv):
        self.send, self.recv, self.at, self.copies = send, recv, 0, []

    def start(self, src, dst, device):
        copy = pltpu.make_async_remote_copy(
            src_ref=src,
            dst_ref=dst,
            send_sem=self.send.at[self.at],
            recv_sem=self.recv.at[self.at],
            device_id=device,
            device_id_type=MESH,
        )
        self.at += 1
        copy.start()
        self.copies.append(copy)
        return copy

    def drain(self):
        for copy in self.copies:
            copy.wait_send()


class Small:
    def __init__(self, place, links, refs, reverse):
        self.p, self.l, self.reverse = place, links, reverse
        self.own, self.rc, self.sz, self.rz, self.sy, self.ry, self.sx, self.rx, self.inc, self.out = refs

    def s0(self):
        self.w = [self.l.start(self.own, self.rc, self.p.core())]

    def wait(self):
        for w in self.w:
            w.wait_recv()

    def s1(self):
        self.wait()
        self.sz[...] = self.own[...] + self.rc[...]
        self.w = [self.l.start(self.sz, self.rz.at[j - 1], self.p.along_z(j)) for j in (1, 2, 3)]

    def s2(self):
        self.wait()
        self.sy[...] = self.sz[...] + self.rz[0] + self.rz[1] + self.rz[2]
        self.w = [self.l.start(self.sy, self.ry.at[j - 1], self.p.along_y(j)) for j in (1, 2, 3)]

    def s3(self):
        self.wait()
        total = self.sy[...]
        part = total
        for j in (1, 2, 3):
            term = self.ry[j - 1]
            total = total + term
            part = part + jnp.where(self.p.earlier(self.p.y, j, self.reverse), term, 0.0)
        self.sx[...] = total
        self.inc[...] = part
        self.w = [self.l.start(self.sx, self.rx.at[j - 1], self.p.along_x(j)) for j in (1, 2, 3)]

    def s4(self):
        self.wait()
        part = self.inc[...]
        for j in (1, 2, 3):
            part = part + jnp.where(self.p.earlier(self.p.x, j, self.reverse), self.rx[j - 1], 0.0)
        self.out[...] = part.astype(BF16).astype(F32)


class Big:
    def __init__(self, place, links, refs, reverse):
        self.p, self.l, self.reverse = place, links, reverse
        self.acc, self.sc, self.rc, self.sz, self.rz, self.sy, self.ry, self.sx, self.rx, self.inc, self.out = refs

    def put(self, i, both):
        both = jnp.concatenate([both, jnp.zeros((2 * HEAD, WIDE - HEAD), F32)], axis=1)
        own, other = both[:HEAD], both[HEAD:]
        first = self.p.c == 0
        rows = slice(i * HEAD, (i + 1) * HEAD)
        self.acc[rows, :] = jnp.where(first, own, other)
        self.sc[rows, :] = jnp.where(first, other, own).astype(BF16)

    def clear(self):
        rows = slice(PER * HEAD, ROWS)
        self.acc[rows, :] = jnp.zeros((ROWS - PER * HEAD, WIDE), F32)
        self.sc[rows, :] = jnp.zeros((ROWS - PER * HEAD, WIDE), BF16)

    def pair(self, i):
        rows = slice(i * HEAD, (i + 1) * HEAD)
        return self.out[0, rows, :], self.out[1, rows, :]

    def wait(self):
        for w in self.w:
            w.wait_recv()

    def s0(self):
        self.w = [self.l.start(self.sc, self.rc, self.p.core())]

    def s1(self):
        self.wait()
        for q in range(RING):
            rows = slice(q * QUARTER, (q + 1) * QUARTER)
            total = self.acc[rows, :] + self.rc[rows, :].astype(F32)
            self.acc[rows, :] = total
            self.sz[q] = total.astype(BF16)
        self.w = [
            self.l.start(self.sz.at[(self.p.z + j) % RING], self.rz.at[j - 1], self.p.along_z(j))
            for j in (1, 2, 3)
        ]

    def s2(self):
        self.wait()
        mine = self.acc[pl.ds(pl.multiple_of(self.p.z * QUARTER, 16), QUARTER), :]
        total = mine + self.rz[0].astype(F32) + self.rz[1].astype(F32) + self.rz[2].astype(F32)
        self.inc[...] = total
        self.sy[...] = total.astype(BF16)
        self.w = [self.l.start(self.sy, self.ry.at[j - 1], self.p.along_y(j)) for j in (1, 2, 3)]

    def s3(self):
        self.wait()
        total = self.inc[...]
        part = total
        for j in (1, 2, 3):
            term = self.ry[j - 1].astype(F32)
            total = total + term
            part = part + jnp.where(self.p.earlier(self.p.y, j, self.reverse), term, 0.0)
        self.inc[...] = part
        self.sx[...] = total.astype(BF16)
        self.w = [self.l.start(self.sx, self.rx.at[j - 1], self.p.along_x(j)) for j in (1, 2, 3)]

    def piece(self, clip, quarter):
        return self.out.at[clip, pl.ds(pl.multiple_of(quarter * QUARTER, 16), QUARTER), :]

    def s4(self):
        self.wait()
        part = self.inc[...]
        for j in (1, 2, 3):
            part = part + jnp.where(
                self.p.earlier(self.p.x, j, self.reverse), self.rx[j - 1].astype(F32), 0.0
            )
        here = self.piece(self.p.c, self.p.z)
        here[...] = part.astype(BF16)
        self.w = [self.l.start(here, here, self.p.along_z(j)) for j in (1, 2, 3)]
        self.wc = [self.l.start(here, here, self.p.core())]

    def s5(self):
        for j in (1, 2, 3):
            self.w[j - 1].wait_recv()
            here = self.piece(self.p.c, (self.p.z - j + RING) % RING)
            self.wc.append(self.l.start(here, here, self.p.core()))

    def s6(self):
        for w in self.wc:
            w.wait_recv()


def small_scratch():
    one = pltpu.VMEM((NROWS, WIDE), F32)
    three = pltpu.VMEM((3, NROWS, WIDE), F32)
    return [one, one, one, three, one, three, one, three, one, one]


def big_scratch():
    three = pltpu.VMEM((3, QUARTER, WIDE), BF16)
    one = pltpu.VMEM((QUARTER, WIDE), BF16)
    return [
        pltpu.VMEM((ROWS, WIDE), F32),
        pltpu.VMEM((ROWS, WIDE), BF16),
        pltpu.VMEM((ROWS, WIDE), BF16),
        pltpu.VMEM((RING, QUARTER, WIDE), BF16),
        three,
        one,
        three,
        one,
        three,
        pltpu.VMEM((QUARTER, WIDE), F32),
        pltpu.VMEM((2, ROWS, WIDE), BF16),
    ]


COPIES = 2 * 10 + 2 * GROUPS * 17
SPANS = ((1024, 1664), (1664, 2304), (2304, 2816), (2816, COLS), (0, 640), (640, 1024))


def row_of(h):
    return slice(h * HEAD, (h + 1) * HEAD)


def in_head(rows):
    shape = (rows, HD)
    lane = lax.broadcasted_iota(jnp.int32, shape, 1)
    low = lax.broadcasted_iota(jnp.int32, shape, 0) * HEAD
    return jnp.logical_and(lane >= low, lane < low + HEAD)


def kernel(
    x_hbm, w_hbm, clip_hbm, og_hbm, att_hbm, ig_hbm,
    xv, wv, clipv, og, feat, ng, inv, dgs, grads, acc, outv, attv, ncol, dcol,
    lsem, send, recv, *rest,
):
    ns, ds_ = rest[:10], rest[10:20]
    bigs = [rest[20 + 11 * i : 31 + 11 * i] for i in range(2 * GROUPS)]
    p = Place()
    barrier = pltpu.get_barrier_semaphore()
    peers = p.peers()
    for peer in peers:
        pl.semaphore_signal(barrier, inc=1, device_id=peer, device_id_type=MESH)

    loads = {
        "clip": pltpu.make_async_copy(clip_hbm, clipv, lsem.at[0]),
        "x": pltpu.make_async_copy(x_hbm.at[0], xv, lsem.at[1]),
        "og": pltpu.make_async_copy(og_hbm.at[0], og, lsem.at[2]),
    }
    for i, (lo, hi) in enumerate(SPANS):
        loads[lo] = pltpu.make_async_copy(w_hbm.at[:, lo:hi], wv.at[:, lo:hi], lsem.at[3 + i])
    for name in ("clip", "x", 1024, 1664, 2304, 2816, 0, 640, "og"):
        loads[name].start()

    links = Links(send, recv)
    norm = Small(p, links, ns, False)
    dnorm = Small(p, links, ds_, True)
    state = [Big(p, links, bigs[g], False) for g in range(GROUPS)]
    grad = [Big(p, links, bigs[GROUPS + g], True) for g in range(GROUPS)]

    def project(lo, hi):
        r = tn(wv[:, lo:hi], xv[...])
        pos = min(max(2 * HD - lo, 0), hi - lo)
        if pos:
            feat[lo : lo + pos, :] = jnp.maximum(r[:pos], 0.0).astype(BF16)
        if pos < hi - lo:
            feat[lo + pos : hi, :] = r[pos:].astype(BF16)

    for b in state + grad:
        b.clear()
    loads["clip"].wait()
    is1 = clipv[...] > 0
    m1 = clipv[...].astype(F32)
    m0 = 1.0 - m1
    m0b, m1b = m0.astype(BF16), m1.astype(BF16)

    def split(v, gap=0):
        parts = [v * m0b, v * m1b]
        if gap:
            zero = jnp.zeros((gap, TOK), BF16)
            parts = [parts[0], zero, parts[1], zero]
        return jnp.concatenate(parts, axis=0)

    def put_rows(ref, r):
        ref[...] = jnp.zeros_like(ref)
        for t in range(TILES):
            width = min(WIDE, HD - t * WIDE)
            ref[2 * t : 2 * t + 2, :width] = r[0:2, t * WIDE : t * WIDE + width]

    def get_rows(ref):
        return jnp.concatenate([ref[2 * t : 2 * t + 2, :] for t in range(TILES)], axis=1)

    def columns(ref, dst):
        for t in range(TILES):
            both = ref[2 * t : 2 * t + 2, :]
            both = jnp.concatenate([both, jnp.zeros((6, WIDE), F32)], axis=0)
            dst[t * WIDE : (t + 1) * WIDE, :] = both.T

    def pick(col, h):
        c = col[row_of(h), :]
        return jnp.where(is1, c[:, 1:2], c[:, 0:1])

    def norm_local():
        side = jnp.concatenate([m0b, m1b, jnp.zeros((14, TOK), BF16)], axis=0)
        put_rows(norm.own, nt(side, feat[HD : 2 * HD, :]))

    def state_local(g):
        for i in range(PER):
            h = g * PER + i
            k, v = feat[row_of(HEADS + h), :], feat[row_of(2 * HEADS + h), :]
            state[g].put(i, nt(split(k), v))

    def denominators():
        rows = get_rows(norm.out)[:, :HD]
        keep = in_head(16)
        side = jnp.concatenate(
            [jnp.where(keep, jnp.broadcast_to(rows[c : c + 1], (16, HD)), 0.0) for c in (0, 1)], axis=0
        )
        den = nn(side.astype(BF16), feat[:HD, :])
        inv[...] = 1.0 / (jnp.where(is1, den[16:], den[:16]) + EPS)
        columns(norm.out, ncol)

    def grad_local(g):
        for i in range(PER):
            h = g * PER + i
            v = (og[row_of(h), :].astype(F32) * inv[h : h + 1, :]).astype(BF16)
            ng[row_of(h), :] = v
            grad[g].put(i, nt(split(feat[row_of(h), :]), v))

    def attend(g):
        for i in range(PER):
            h = g * PER + i
            q = feat[row_of(h), :]
            s0, s1 = state[g].pair(i)
            r = inv[h : h + 1, :]
            att = tn(jnp.concatenate([s0, s1], axis=0), split(q))[:HEAD] * r
            attv[row_of(h), :] = att.astype(BF16)
            d = -jnp.sum(og[row_of(h), :].astype(F32) * att, axis=0, keepdims=True) * r
            dgs[h : h + 1, :] = d
            qg = nn(jnp.concatenate([s0, s1], axis=1), split(ng[row_of(h), :], WIDE - HEAD))
            qg = qg + d * pick(ncol, h)
            grads[row_of(h), :] = jnp.where(q.astype(F32) > 0, qg, 0.0).astype(BF16)

    def dnorm_local():
        d = dgs[...]
        both = jnp.concatenate([d * m0, d * m1], axis=0)
        hi = both.astype(BF16)
        lo = (both - hi.astype(F32)).astype(BF16)
        r = nt(jnp.concatenate([hi, lo], axis=0), feat[:HD, :])
        r = r[:32] + r[32:]
        keep = in_head(16)
        rows = [
            jnp.sum(jnp.where(keep, r[16 * c : 16 * c + 16], 0.0), axis=0, keepdims=True) for c in (0, 1)
        ]
        put_rows(dnorm.own, jnp.concatenate(rows, axis=0))

    def value_grads(g):
        for i in range(PER):
            h = g * PER + i
            g0, g1 = grad[g].pair(i)
            r = tn(jnp.concatenate([g0, g1], axis=0), split(feat[row_of(HEADS + h), :]))
            grads[row_of(2 * HEADS + h), :] = r[:HEAD].astype(BF16)

    def key_grads(g):
        for i in range(PER):
            h = g * PER + i
            g0, g1 = grad[g].pair(i)
            v = feat[row_of(2 * HEADS + h), :]
            kg = nn(jnp.concatenate([g0, g1], axis=1), split(v, WIDE - HEAD)) + pick(dcol, h)
            keep = feat[row_of(HEADS + h), :].astype(F32) > 0
            grads[row_of(HEADS + h), :] = jnp.where(keep, kg, 0.0).astype(BF16)

    def back(lo, hi, kind, then=None):
        for m in (0, 1):
            rows = slice(m * HD, (m + 1) * HD)
            r = nn(wv[rows, lo:hi], grads[lo:hi, :])
            if kind > 0:
                r = r + acc[rows, :]
            if kind < 2:
                acc[rows, :] = r
            else:
                outv[rows, :] = r.astype(BF16)
                then(m, rows)

    stores = []

    def store(src, dst, at):
        stores.append(pltpu.make_async_copy(src, dst, lsem.at[at]))
        stores[-1].start()

    loads["x"].wait()
    for lo, hi in SPANS[:2]:
        loads[lo].wait()
        project(lo, hi)
    norm_local()
    pl.semaphore_wait(barrier, len(peers))
    norm.s0()
    loads[2304].wait()
    project(2304, 2816)
    norm.s1()
    state_local(0)
    state[0].s0()
    loads[2816].wait()
    project(2816, COLS)
    norm.s2()
    state[0].s1()
    state_local(1)
    state[1].s0()
    loads[0].wait()
    project(0, 640)
    norm.s3()
    state[1].s1()
    state[0].s2()
    loads[640].wait()
    project(640, 1024)
    state[1].s2()
    norm.s4()
    loads["og"].wait()
    denominators()
    state[0].s3()
    grad_local(0)
    grad[0].s0()
    state[1].s3()
    grad_local(1)
    grad[1].s0()
    grad[0].s1()
    state[0].s4()
    grad[1].s1()
    state[1].s4()
    grad[0].s2()
    state[0].s5()
    grad[1].s2()
    state[1].s5()
    grad[0].s3()
    state[0].s6()
    attend(0)
    grad[1].s3()
    state[1].s6()
    attend(1)
    store(attv, att_hbm.at[0], 0)
    dnorm_local()
    dnorm.s0()
    grad[0].s4()
    grad[1].s4()
    dnorm.s1()
    grad[0].s5()
    grad[1].s5()
    back(0, 1024, 0)
    dnorm.s2()
    grad[0].s6()
    value_grads(0)
    grad[1].s6()
    dnorm.s3()
    value_grads(1)
    back(2304, COLS, 1)
    dnorm.s4()
    columns(dnorm.out, dcol)
    key_grads(0)
    key_grads(1)
    back(1024, 2304, 2, lambda m, rows: store(outv.at[rows, :], ig_hbm.at[0, rows, :], 1 + m))
    links.drain()
    for s in stores:
        s.wait()


def per_device(inputs, weight, clip_of_row, out_grad):
    anywhere = pl.BlockSpec(memory_space=pl.ANY)
    bigs = [r for _ in range(2 * GROUPS) for r in big_scratch()]
    att, grad = pl.pallas_call(
        kernel,
        out_shape=(
            jax.ShapeDtypeStruct((1, HD, TOK), BF16),
            jax.ShapeDtypeStruct((1, D, TOK), BF16),
        ),
        in_specs=[anywhere] * 4,
        out_specs=(anywhere, anywhere),
        scratch_shapes=[
            pltpu.VMEM((D, TOK), BF16),
            pltpu.VMEM((D, COLS), BF16),
            pltpu.VMEM((1, TOK), jnp.int32),
            pltpu.VMEM((HD, TOK), BF16),
            pltpu.VMEM((COLS, TOK), BF16),
            pltpu.VMEM((HD, TOK), BF16),
            pltpu.VMEM((16, TOK), F32),
            pltpu.VMEM((16, TOK), F32),
            pltpu.VMEM((COLS, TOK), BF16),
            pltpu.VMEM((D, TOK), F32),
            pltpu.VMEM((D, TOK), BF16),
            pltpu.VMEM((HD, TOK), BF16),
            pltpu.VMEM((TILES * WIDE, 8), F32),
            pltpu.VMEM((TILES * WIDE, 8), F32),
            pltpu.SemaphoreType.DMA((9,)),
            pltpu.SemaphoreType.DMA((COPIES,)),
            pltpu.SemaphoreType.DMA((COPIES,)),
            *small_scratch(),
            *small_scratch(),
            *bigs,
        ],
        compiler_params=pltpu.CompilerParams(
            collective_id=0, has_side_effects=True, vmem_limit_bytes=67000000
        ),
    )(inputs.swapaxes(1, 2), weight, clip_of_row, out_grad.swapaxes(1, 2))
    return att.swapaxes(1, 2), grad.swapaxes(1, 2)


def solution(mesh):
    placed = (P("frame", "pack", None), P(), P("frame", "pack"), P("frame", "pack", None))
    return jax.shard_map(
        per_device,
        mesh=mesh,
        in_specs=placed,
        out_specs=(P("frame", "pack", None), P("frame", "pack", None)),
        check_vma=False,
    )
```

time: 94.7 us -> 69 us (0.73)
  Pallas kernels: 82.2 us -> 64.4 us
  local copies, waits for them, and re-layouts: 11.7 us -> 3.87 us
    pallas_call x1, Pallas kernels: 82.2 us -> 64.4 us  [per_device(): pl.pallas_call(kernel, out_shape=(jax.ShapeDtypeStruct((1, HD, TOK), BF16...]
    pallas_call x2 -> x0, local copies, waits for them, and re-layouts: 6.61 us -> none  [per_device(): pl.pallas_call(kernel, out_shape=(jax.ShapeDtypeStruct((1, TOK, HD), BF16...]
    unnamed x4, local copies, waits for them, and re-layouts: 5.07 us -> 3.87 us
where the time goes in v2:
time: 69 us; the launch traced here: 68.9 us
  Pallas kernels  64.4 us (93%)
  local copies, waits for them, and re-layouts  3.87 us (6%)
    pallas_call x1, Pallas kernels, per_device(): pl.pallas_call(kernel, out_shape=(jax.ShapeDtypeStruct((1, HD, TOK), BF16...  64.4 us
    unnamed x4, local copies, waits for them, and re-layouts  3.87 us

profile of v2, /device:TPU:0, one launch (start us, length us, event | category | flops | bytes accessed | tf_op | source)
XLA Modules:
  0.0 68.9 jit_solution(15881708845645916306)
XLA Ops:
  0.6 64.4 %shard_map.59 = (bf16[1,1120,512]{2,1,0:T(8,128)(2,1)}, bf16[1,2240,512]{2,1,0:T(8,128)(2,1)}) custom-call(bf16[1,2240,512]{2,1,0:T(8,128)(2,1)} %bitcast.5, bf16[2240,3360]{1,0:T(8,128)(2,1)} %w_hbm.1, s32[1,512]{1,0:T(1,128)} %clip_hbm.1, bf16[1,1120,512]{2,1,0:T(8,128)(2,1)} %bitcast.6), custom_call_target="tpu_custom_call" | custom-call | tf_op jit(solution)/shard_map/pallas_call | solution.py:498
  65.0 0.0 copy-start
  65.0 2.5 %copy.8 = bf16[1,512,1120]{1,2,0:T(8,128)(2,1)} copy(bf16[1,512,1120]{1,2,0:T(8,128)(2,1)} %bitcast.7) | data formatting | bytes 2293760
  67.5 0.0 copy-done
  67.5 1.4 %copy.9 = bf16[1,512,2240]{1,2,0:T(8,128)(2,1)} copy(bf16[1,512,2240]{1,2,0:T(8,128)(2,1)S(1)} %bitcast.4) | data formatting | bytes 4587520
Async XLA Ops:
  65.0 2.5 %copy-start = (bf16[1,2240,512]{2,1,0:T(8,128)(2,1)S(1)}, bf16[1,2240,512]{2,1,0:T(8,128)(2,1)}, u32[]{:S(2)}) copy-start(bf16[1,2240,512]{2,1,0:T(8,128)(2,1)} %get-tuple-element.5) | copy-start | bytes 6881284

commit v3 on v2

--- a/solution.py
+++ b/solution.py
@@ -17,6 +17,8 @@
 HD = HEADS * HEAD
 COLS = 3 * HD
 RING = 4
+PACK = 2 * RING
+FRAMES = RING * RING
 GROUPS = 2
 PER = HEADS // GROUPS
 ROWS = 576
@@ -39,39 +41,30 @@
 
 class Place:
     def __init__(self):
-        frame = lax.axis_index("frame")
-        pack = lax.axis_index("pack")
-        self.x, self.y = frame // RING, frame % RING
-        self.z, self.c = pack // 2, pack % 2
-        self.frame, self.pack = frame, pack
-
-    def core(self):
-        return {"frame": self.frame, "pack": self.z * 2 + (1 - self.c)}
-
-    def along_z(self, j):
-        return {"frame": self.frame, "pack": ((self.z + j) % RING) * 2 + self.c}
-
-    def along_y(self, j):
-        return {"frame": self.x * RING + (self.y + j) % RING, "pack": self.pack}
-
-    def along_x(self, j):
-        return {"frame": ((self.x + j) % RING) * RING + self.y, "pack": self.pack}
+        self.frame = lax.axis_index("frame")
+        self.pack = lax.axis_index("pack")
+        self.z, self.c = self.pack // 2, self.pack % 2
+
+    def pack_peer(self, k):
+        dz, flip = divmod(k + 1, 2)
+        z = (self.z + dz) % RING
+        c = (self.c + flip) % 2
+        return {"frame": self.frame, "pack": z * 2 + c}, z, c
+
+    def frame_peer(self, j):
+        return {"frame": (self.frame + j + FRAMES) % FRAMES, "pack": self.pack}
 
     def peers(self):
-        out = [self.core()]
-        for j in (1, 2, 3):
-            out += [self.along_z(j), self.along_y(j), self.along_x(j)]
-        return out
-
-    def earlier(self, at, j, reverse):
-        return (j > at) if reverse else (j <= at)
+        return [self.pack_peer(k)[0] for k in range(PACK - 1)] + [
+            self.frame_peer(j) for j in range(1, FRAMES)
+        ]
 
 
 class Links:
     def __init__(self, send, recv):
         self.send, self.recv, self.at, self.copies = send, recv, 0, []
 
-    def start(self, src, dst, device):
+    def start(self, src, dst, device, when=None):
         copy = pltpu.make_async_remote_copy(
             src_ref=src,
             dst_ref=dst,
@@ -81,169 +74,133 @@
             device_id_type=MESH,
         )
         self.at += 1
-        copy.start()
-        self.copies.append(copy)
+        if when is None:
+            copy.start()
+        else:
+            pl.when(when)(copy.start)
+        self.copies.append((copy, when))
         return copy
 
     def drain(self):
-        for copy in self.copies:
-            copy.wait_send()
-
-
-class Small:
+        for copy, when in self.copies:
+            if when is None:
+                copy.wait_send()
+            else:
+                pl.when(when)(copy.wait_send)
+
+
+class Frames:
+    def __init__(self, place, links, reverse):
+        self.p, self.l, self.reverse = place, links, reverse
+
+    def spread(self, src, slots):
+        f = self.p.frame
+        self.w = []
+        for j in range(1, FRAMES):
+            to, into = (f >= j, f + j < FRAMES) if self.reverse else (f + j < FRAMES, f >= j)
+            peer = self.p.frame_peer(-j if self.reverse else j)
+            self.w.append((self.l.start(src, slots.at[j - 1], peer, to), into))
+
+    def total(self, own, slots):
+        for copy, into in self.w:
+            pl.when(into)(copy.wait_recv)
+        for j, (_, into) in enumerate(self.w):
+            own = own + jnp.where(into, slots[j].astype(F32), 0.0)
+        return own
+
+
+class Small(Frames):
     def __init__(self, place, links, refs, reverse):
-        self.p, self.l, self.reverse = place, links, reverse
-        self.own, self.rc, self.sz, self.rz, self.sy, self.ry, self.sx, self.rx, self.inc, self.out = refs
+        super().__init__(place, links, reverse)
+        self.own, self.rz, self.sy, self.ry, self.out = refs
 
     def s0(self):
-        self.w = [self.l.start(self.own, self.rc, self.p.core())]
-
-    def wait(self):
-        for w in self.w:
+        self.wp = [
+            self.l.start(self.own, self.rz.at[k], self.p.pack_peer(k)[0]) for k in range(PACK - 1)
+        ]
+
+    def s1(self):
+        for w in self.wp:
             w.wait_recv()
-
-    def s1(self):
-        self.wait()
-        self.sz[...] = self.own[...] + self.rc[...]
-        self.w = [self.l.start(self.sz, self.rz.at[j - 1], self.p.along_z(j)) for j in (1, 2, 3)]
+        total = self.own[...]
+        for k in range(PACK - 1):
+            total = total + self.rz[k]
+        self.sy[...] = total
+        self.spread(self.sy, self.ry)
 
     def s2(self):
-        self.wait()
-        self.sy[...] = self.sz[...] + self.rz[0] + self.rz[1] + self.rz[2]
-        self.w = [self.l.start(self.sy, self.ry.at[j - 1], self.p.along_y(j)) for j in (1, 2, 3)]
-
-    def s3(self):
-        self.wait()
-        total = self.sy[...]
-        part = total
-        for j in (1, 2, 3):
-            term = self.ry[j - 1]
-            total = total + term
-            part = part + jnp.where(self.p.earlier(self.p.y, j, self.reverse), term, 0.0)
-        self.sx[...] = total
-        self.inc[...] = part
-        self.w = [self.l.start(self.sx, self.rx.at[j - 1], self.p.along_x(j)) for j in (1, 2, 3)]
-
-    def s4(self):
-        self.wait()
-        part = self.inc[...]
-        for j in (1, 2, 3):
-            part = part + jnp.where(self.p.earlier(self.p.x, j, self.reverse), self.rx[j - 1], 0.0)
-        self.out[...] = part.astype(BF16).astype(F32)
-
-
-class Big:
+        self.out[...] = self.total(self.sy[...], self.ry).astype(BF16).astype(F32)
+
+
+class Big(Frames):
     def __init__(self, place, links, refs, reverse):
-        self.p, self.l, self.reverse = place, links, reverse
-        self.acc, self.sc, self.rc, self.sz, self.rz, self.sy, self.ry, self.sx, self.rx, self.inc, self.out = refs
+        super().__init__(place, links, reverse)
+        self.acc, self.sz, self.rz, self.inc, self.sy, self.ry, self.out = refs
 
     def put(self, i, both):
         both = jnp.concatenate([both, jnp.zeros((2 * HEAD, WIDE - HEAD), F32)], axis=1)
-        own, other = both[:HEAD], both[HEAD:]
-        first = self.p.c == 0
         rows = slice(i * HEAD, (i + 1) * HEAD)
-        self.acc[rows, :] = jnp.where(first, own, other)
-        self.sc[rows, :] = jnp.where(first, other, own).astype(BF16)
+        self.acc[rows, :] = jnp.where(self.p.c == 0, both[:HEAD], both[HEAD:])
+        self.sz[0, rows, :] = both[:HEAD].astype(BF16)
+        self.sz[1, rows, :] = both[HEAD:].astype(BF16)
 
     def clear(self):
         rows = slice(PER * HEAD, ROWS)
         self.acc[rows, :] = jnp.zeros((ROWS - PER * HEAD, WIDE), F32)
-        self.sc[rows, :] = jnp.zeros((ROWS - PER * HEAD, WIDE), BF16)
+        for c in (0, 1):
+            self.sz[c, rows, :] = jnp.zeros((ROWS - PER * HEAD, WIDE), BF16)
 
     def pair(self, i):
         rows = slice(i * HEAD, (i + 1) * HEAD)
         return self.out[0, rows, :], self.out[1, rows, :]
 
-    def wait(self):
-        for w in self.w:
+    def quarter(self, z):
+        return pl.ds(pl.multiple_of(z * QUARTER, 16), QUARTER)
+
+    def s0(self):
+        self.wp = []
+        for k in range(PACK - 1):
+            peer, z, c = self.p.pack_peer(k)
+            self.wp.append(self.l.start(self.sz.at[c, self.quarter(z), :], self.rz.at[k], peer))
+
+    def s1(self):
+        for w in self.wp:
             w.wait_recv()
-
-    def s0(self):
-        self.w = [self.l.start(self.sc, self.rc, self.p.core())]
-
-    def s1(self):
-        self.wait()
-        for q in range(RING):
-            rows = slice(q * QUARTER, (q + 1) * QUARTER)
-            total = self.acc[rows, :] + self.rc[rows, :].astype(F32)
-            self.acc[rows, :] = total
-            self.sz[q] = total.astype(BF16)
-        self.w = [
-            self.l.start(self.sz.at[(self.p.z + j) % RING], self.rz.at[j - 1], self.p.along_z(j))
-            for j in (1, 2, 3)
-        ]
-
-    def s2(self):
-        self.wait()
-        mine = self.acc[pl.ds(pl.multiple_of(self.p.z * QUARTER, 16), QUARTER), :]
-        total = mine + self.rz[0].astype(F32) + self.rz[1].astype(F32) + self.rz[2].astype(F32)
+        total = self.acc[self.quarter(self.p.z), :]
+        for k in range(PACK - 1):
+            total = total + self.rz[k].astype(F32)
         self.inc[...] = total
         self.sy[...] = total.astype(BF16)
-        self.w = [self.l.start(self.sy, self.ry.at[j - 1], self.p.along_y(j)) for j in (1, 2, 3)]
+        self.spread(self.sy, self.ry)
+
+    def s2(self):
+        here = self.out.at[self.p.c, self.quarter(self.p.z), :]
+        here[...] = self.total(self.inc[...], self.ry).astype(BF16)
+        self.wp = [self.l.start(here, here, self.p.pack_peer(k)[0]) for k in range(PACK - 1)]
 
     def s3(self):
-        self.wait()
-        total = self.inc[...]
-        part = total
-        for j in (1, 2, 3):
-            term = self.ry[j - 1].astype(F32)
-            total = total + term
-            part = part + jnp.where(self.p.earlier(self.p.y, j, self.reverse), term, 0.0)
-        self.inc[...] = part
-        self.sx[...] = total.astype(BF16)
-        self.w = [self.l.start(self.sx, self.rx.at[j - 1], self.p.along_x(j)) for j in (1, 2, 3)]
-
-    def piece(self, clip, quarter):
-        return self.out.at[clip, pl.ds(pl.multiple_of(quarter * QUARTER, 16), QUARTER), :]
-
-    def s4(self):
-        self.wait()
-        part = self.inc[...]
-        for j in (1, 2, 3):
-            part = part + jnp.where(
-                self.p.earlier(self.p.x, j, self.reverse), self.rx[j - 1].astype(F32), 0.0
-            )
-        here = self.piece(self.p.c, self.p.z)
-        here[...] = part.astype(BF16)
-        self.w = [self.l.start(here, here, self.p.along_z(j)) for j in (1, 2, 3)]
-        self.wc = [self.l.start(here, here, self.p.core())]
-
-    def s5(self):
-        for j in (1, 2, 3):
-            self.w[j - 1].wait_recv()
-            here = self.piece(self.p.c, (self.p.z - j + RING) % RING)
-            self.wc.append(self.l.start(here, here, self.p.core()))
-
-    def s6(self):
-        for w in self.wc:
+        for w in self.wp:
             w.wait_recv()
 
 
 def small_scratch():
     one = pltpu.VMEM((NROWS, WIDE), F32)
-    three = pltpu.VMEM((3, NROWS, WIDE), F32)
-    return [one, one, one, three, one, three, one, three, one, one]
+    return [one, pltpu.VMEM((PACK - 1, NROWS, WIDE), F32), one, pltpu.VMEM((FRAMES - 1, NROWS, WIDE), F32), one]
 
 
 def big_scratch():
-    three = pltpu.VMEM((3, QUARTER, WIDE), BF16)
-    one = pltpu.VMEM((QUARTER, WIDE), BF16)
     return [
         pltpu.VMEM((ROWS, WIDE), F32),
-        pltpu.VMEM((ROWS, WIDE), BF16),
-        pltpu.VMEM((ROWS, WIDE), BF16),
-        pltpu.VMEM((RING, QUARTER, WIDE), BF16),
-        three,
-        one,
-        three,
-        one,
-        three,
+        pltpu.VMEM((2, ROWS, WIDE), BF16),
+        pltpu.VMEM((PACK - 1, QUARTER, WIDE), BF16),
         pltpu.VMEM((QUARTER, WIDE), F32),
+        pltpu.VMEM((QUARTER, WIDE), BF16),
+        pltpu.VMEM((FRAMES - 1, QUARTER, WIDE), BF16),
         pltpu.VMEM((2, ROWS, WIDE), BF16),
     ]
 
 
-COPIES = 2 * 10 + 2 * GROUPS * 17
+COPIES = 2 * (PACK - 1 + FRAMES - 1) + 2 * GROUPS * (2 * (PACK - 1) + FRAMES - 1)
 SPANS = ((1024, 1664), (1664, 2304), (2304, 2816), (2816, COLS), (0, 640), (640, 1024))
 
 
@@ -263,8 +220,8 @@
     xv, wv, clipv, og, feat, ng, inv, dgs, grads, acc, outv, attv, ncol, dcol,
     lsem, send, recv, *rest,
 ):
-    ns, ds_ = rest[:10], rest[10:20]
-    bigs = [rest[20 + 11 * i : 31 + 11 * i] for i in range(2 * GROUPS)]
+    ns, ds_ = rest[:5], rest[5:10]
+    bigs = [rest[10 + 7 * i : 17 + 7 * i] for i in range(2 * GROUPS)]
     p = Place()
     barrier = pltpu.get_barrier_semaphore()
     peers = p.peers()
@@ -278,7 +235,7 @@
     }
     for i, (lo, hi) in enumerate(SPANS):
         loads[lo] = pltpu.make_async_copy(w_hbm.at[:, lo:hi], wv.at[:, lo:hi], lsem.at[3 + i])
-    for name in ("clip", "x", 1024, 1664, 2304, 2816, 0, 640, "og"):
+    for name in ("clip", "x", 1024):
         loads[name].start()
 
     links = Links(send, recv)
@@ -418,71 +375,62 @@
         stores[-1].start()
 
     loads["x"].wait()
-    for lo, hi in SPANS[:2]:
-        loads[lo].wait()
-        project(lo, hi)
+    loads[1024].wait()
+    loads[1664].start()
+    loads[2304].start()
+    project(1024, 1664)
+    loads[1664].wait()
+    loads[2816].start()
+    loads[0].start()
+    project(1664, 2304)
     norm_local()
     pl.semaphore_wait(barrier, len(peers))
     norm.s0()
     loads[2304].wait()
+    loads[640].start()
+    loads["og"].start()
     project(2304, 2816)
-    norm.s1()
     state_local(0)
     state[0].s0()
     loads[2816].wait()
     project(2816, COLS)
-    norm.s2()
-    state[0].s1()
+    norm.s1()
     state_local(1)
     state[1].s0()
     loads[0].wait()
     project(0, 640)
-    norm.s3()
-    state[1].s1()
-    state[0].s2()
+    state[0].s1()
     loads[640].wait()
     project(640, 1024)
-    state[1].s2()
-    norm.s4()
+    norm.s2()
     loads["og"].wait()
     denominators()
-    state[0].s3()
     grad_local(0)
     grad[0].s0()
-    state[1].s3()
+    state[1].s1()
     grad_local(1)
     grad[1].s0()
+    state[0].s2()
     grad[0].s1()
-    state[0].s4()
+    state[1].s2()
     grad[1].s1()
-    state[1].s4()
+    state[0].s3()
+    attend(0)
     grad[0].s2()
-    state[0].s5()
-    grad[1].s2()
-    state[1].s5()
-    grad[0].s3()
-    state[0].s6()
-    attend(0)
-    grad[1].s3()
-    state[1].s6()
+    state[1].s3()
     attend(1)
-    store(attv, att_hbm.at[0], 0)
     dnorm_local()
     dnorm.s0()
-    grad[0].s4()
-    grad[1].s4()
+    store(attv, att_hbm.at[0], 0)
+    grad[1].s2()
+    back(0, 1024, 0)
     dnorm.s1()
-    grad[0].s5()
-    grad[1].s5()
-    back(0, 1024, 0)
-    dnorm.s2()
-    grad[0].s6()
+    grad[0].s3()
     value_grads(0)
-    grad[1].s6()
-    dnorm.s3()
+    grad[1].s3()
     value_grads(1)
     back(2304, COLS, 1)
-    dnorm.s4()
+    dnorm.s2()
     columns(dnorm.out, dcol)
     key_grads(0)
     key_grads(1)

time: 69 us -> 69.4 us (level)
  the two profiles are of different devices: /device:TPU:0 before, /device:TPU:1 now
where the time goes in v3:
time: 69.4 us; the launch traced here: 68.6 us
  Pallas kernels  64.1 us (92%)
  local copies, waits for them, and re-layouts  3.87 us (6%)
    pallas_call x1, Pallas kernels, per_device(): pl.pallas_call(kernel, out_shape=(jax.ShapeDtypeStruct((1, HD, TOK), BF16...  64.1 us
    unnamed x4, local copies, waits for them, and re-layouts  3.87 us

profile of v3, /device:TPU:1, one launch (start us, length us, event | category | flops | bytes accessed | tf_op | source)
XLA Modules:
  0.0 68.6 jit_solution(2577270426707174200)
XLA Ops:
  0.6 64.1 %shard_map.59 = (bf16[1,1120,512]{2,1,0:T(8,128)(2,1)}, bf16[1,2240,512]{2,1,0:T(8,128)(2,1)}) custom-call(bf16[1,2240,512]{2,1,0:T(8,128)(2,1)} %bitcast.5, bf16[2240,3360]{1,0:T(8,128)(2,1)} %w_hbm.1, s32[1,512]{1,0:T(1,128)} %clip_hbm.1, bf16[1,1120,512]{2,1,0:T(8,128)(2,1)} %bitcast.6), custom_call_target="tpu_custom_call" | custom-call | tf_op jit(solution)/shard_map/pallas_call | solution.py:446
  64.8 0.0 copy-start
  64.8 2.5 %copy.8 = bf16[1,512,1120]{1,2,0:T(8,128)(2,1)} copy(bf16[1,512,1120]{1,2,0:T(8,128)(2,1)} %bitcast.7) | data formatting | bytes 2293760
  67.3 0.0 copy-done
  67.3 1.4 %copy.9 = bf16[1,512,2240]{1,2,0:T(8,128)(2,1)} copy(bf16[1,512,2240]{1,2,0:T(8,128)(2,1)S(1)} %bitcast.4) | data formatting | bytes 4587520
Async XLA Ops:
  64.8 2.5 %copy-start = (bf16[1,2240,512]{2,1,0:T(8,128)(2,1)S(1)}, bf16[1,2240,512]{2,1,0:T(8,128)(2,1)}, u32[]{:S(2)}) copy-start(bf16[1,2240,512]{2,1,0:T(8,128)(2,1)} %get-tuple-element.5) | copy-start | bytes 6881284

commit v4 on v3

--- a/solution.py
+++ b/solution.py
@@ -19,10 +19,10 @@
 RING = 4
 PACK = 2 * RING
 FRAMES = RING * RING
-GROUPS = 2
-PER = HEADS // GROUPS
-ROWS = 576
-QUARTER = ROWS // RING
+CHIPS = RING * FRAMES
+PIECE = 16
+ROWS = CHIPS * PIECE
+SPARE = WIDE - HEAD
 NROWS = 24
 TILES = 9
 
@@ -37,27 +37,44 @@
 
 def nn(a, b):
     return lax.dot_general(a, b, (((1,), (0,)), ((), ())), preferred_element_type=F32)
+
+
+def row_of(h):
+    return slice(h * HEAD, (h + 1) * HEAD)
 
 
 class Place:
     def __init__(self):
         self.frame = lax.axis_index("frame")
         self.pack = lax.axis_index("pack")
+        self.x, self.y = self.frame // RING, self.frame % RING
         self.z, self.c = self.pack // 2, self.pack % 2
+
+    def core_peer(self):
+        return self.pack_peer(0)
+
+    def chip(self, e, sign=1):
+        dz, dx, dy = e // FRAMES, (e % FRAMES) // RING, e % RING
+        x = (self.x + sign * dx + RING) % RING
+        y = (self.y + sign * dy + RING) % RING
+        return x * RING + y, (self.z + sign * dz + RING) % RING
+
+    def chip_peer(self, e):
+        frame, z = self.chip(e)
+        return {"frame": frame, "pack": z * 2 + self.c}
 
     def pack_peer(self, k):
         dz, flip = divmod(k + 1, 2)
         z = (self.z + dz) % RING
         c = (self.c + flip) % 2
-        return {"frame": self.frame, "pack": z * 2 + c}, z, c
+        return {"frame": self.frame, "pack": z * 2 + c}
 
     def frame_peer(self, j):
         return {"frame": (self.frame + j + FRAMES) % FRAMES, "pack": self.pack}
 
     def peers(self):
-        return [self.pack_peer(k)[0] for k in range(PACK - 1)] + [
-            self.frame_peer(j) for j in range(1, FRAMES)
-        ]
+        other = [self.pack_peer(k) for k in range(0, PACK - 1, 2)]
+        return other + [self.chip_peer(e) for e in range(1, CHIPS)]
 
 
 class Links:
@@ -116,7 +133,7 @@
 
     def s0(self):
         self.wp = [
-            self.l.start(self.own, self.rz.at[k], self.p.pack_peer(k)[0]) for k in range(PACK - 1)
+            self.l.start(self.own, self.rz.at[k], self.p.pack_peer(k)) for k in range(PACK - 1)
         ]
 
     def s1(self):
@@ -132,55 +149,103 @@
         self.out[...] = self.total(self.sy[...], self.ry).astype(BF16).astype(F32)
 
 
-class Big(Frames):
-    def __init__(self, place, links, refs, reverse):
-        super().__init__(place, links, reverse)
-        self.acc, self.sz, self.rz, self.inc, self.sy, self.ry, self.out = refs
-
-    def put(self, i, both):
-        both = jnp.concatenate([both, jnp.zeros((2 * HEAD, WIDE - HEAD), F32)], axis=1)
-        rows = slice(i * HEAD, (i + 1) * HEAD)
-        self.acc[rows, :] = jnp.where(self.p.c == 0, both[:HEAD], both[HEAD:])
-        self.sz[0, rows, :] = both[:HEAD].astype(BF16)
-        self.sz[1, rows, :] = both[HEAD:].astype(BF16)
+def lane_of(shape):
+    return lax.broadcasted_iota(jnp.int32, shape, 1)
+
+
+class Big:
+    def __init__(self, place, links, refs, sems, reverse):
+        self.p, self.l, self.reverse, self.sems = place, links, reverse, sems
+        self.acc, self.sc, self.rc, self.sz, self.rz, self.blocks, self.sums, self.out = refs
+
+    def put(self, h, both, last):
+        both = jnp.concatenate([both, jnp.zeros((2 * HEAD, SPARE), F32)], axis=1)
+        if h < HEAD // SPARE:
+            moved = pltpu.roll(last, HEAD - SPARE * h, 1) if SPARE * h < HEAD else last
+            both = jnp.where(lane_of(both.shape) < HEAD, both, moved)
+        first = self.p.c == 0
+        rows = row_of(h)
+        self.acc[rows, :] = jnp.where(first, both[:HEAD], both[HEAD:])
+        self.sc[rows, :] = jnp.where(first, both[HEAD:], both[:HEAD]).astype(BF16)
 
     def clear(self):
-        rows = slice(PER * HEAD, ROWS)
-        self.acc[rows, :] = jnp.zeros((ROWS - PER * HEAD, WIDE), F32)
+        rows = slice((HEADS - 1) * HEAD, ROWS)
+        self.acc[rows, :] = jnp.zeros((PIECE, WIDE), F32)
+        self.sc[rows, :] = jnp.zeros((PIECE, WIDE), BF16)
+
+    def pair(self, h):
+        if h < HEADS - 1:
+            return self.out[0, row_of(h), :], self.out[1, row_of(h), :]
+        found = []
         for c in (0, 1):
-            self.sz[c, rows, :] = jnp.zeros((ROWS - PER * HEAD, WIDE), BF16)
-
-    def pair(self, i):
-        rows = slice(i * HEAD, (i + 1) * HEAD)
-        return self.out[0, rows, :], self.out[1, rows, :]
-
-    def quarter(self, z):
-        return pl.ds(pl.multiple_of(z * QUARTER, 16), QUARTER)
+            whole = jnp.zeros((HEAD, WIDE), F32)
+            lane = lane_of(whole.shape)
+            for i in range(HEAD // SPARE):
+                part = pltpu.roll(self.out[c, row_of(i), :].astype(F32), SPARE * (i + 1), 1)
+                here = jnp.logical_and(lane >= SPARE * i, lane < SPARE * (i + 1))
+                whole = jnp.where(here, part, whole)
+            found.append(whole.astype(BF16))
+        return found
+
+    def piece(self, i):
+        return pl.ds(pl.multiple_of(i * PIECE, PIECE), PIECE)
+
+    def mine(self):
+        return self.piece(self.p.z * FRAMES + self.p.frame)
+
+    def send(self, at, src, dst, peer):
+        pltpu.make_async_remote_copy(
+            src_ref=src,
+            dst_ref=dst,
+            send_sem=self.sems.at[2 * at],
+            recv_sem=self.sems.at[2 * at + 1],
+            device_id=peer,
+            device_id_type=MESH,
+        ).start()
+
+    def wait(self, sem):
+        most = self.sc.at[0 : ROWS - PIECE, :]
+        pltpu.make_async_copy(most, most, self.sems.at[sem]).wait()
 
     def s0(self):
-        self.wp = []
-        for k in range(PACK - 1):
-            peer, z, c = self.p.pack_peer(k)
-            self.wp.append(self.l.start(self.sz.at[c, self.quarter(z), :], self.rz.at[k], peer))
+        self.wp = self.l.start(self.sc, self.rc, self.p.core_peer())
 
     def s1(self):
-        for w in self.wp:
-            w.wait_recv()
-        total = self.acc[self.quarter(self.p.z), :]
-        for k in range(PACK - 1):
-            total = total + self.rz[k].astype(F32)
-        self.inc[...] = total
-        self.sy[...] = total.astype(BF16)
-        self.spread(self.sy, self.ry)
+        self.wp.wait_recv()
+        total = self.acc[...] + self.rc[...].astype(F32)
+        self.acc[...] = total
+        self.sz[...] = total.astype(BF16)
+        for e in range(1, CHIPS):
+            frame, z = self.p.chip(e)
+            self.send(0, self.sz.at[self.piece(z * FRAMES + frame), :], self.rz.at[e - 1], self.p.chip_peer(e))
 
     def s2(self):
-        here = self.out.at[self.p.c, self.quarter(self.p.z), :]
-        here[...] = self.total(self.inc[...], self.ry).astype(BF16)
-        self.wp = [self.l.start(here, here, self.p.pack_peer(k)[0]) for k in range(PACK - 1)]
+        self.wait(1)
+        for d in range(FRAMES):
+            total = self.acc[self.mine(), :] if d == 0 else self.rz[d - 1].astype(F32)
+            for dz in range(1, RING):
+                total = total + self.rz[dz * FRAMES + d - 1].astype(F32)
+            self.blocks[self.p.chip(d, -1)[0]] = total
+        total = jnp.zeros((PIECE, WIDE), F32)
+        for f in reversed(range(FRAMES)) if self.reverse else range(FRAMES):
+            total = total + self.blocks[f]
+            self.sums[f] = total.astype(BF16)
+        here = self.out.at[self.p.c, self.mine(), :]
+        here[...] = self.sums[self.p.frame]
+        for e in range(1, CHIPS):
+            self.send(1, self.sums.at[self.p.chip(e)[0]], here, self.p.chip_peer(e))
 
     def s3(self):
-        for w in self.wp:
-            w.wait_recv()
+        self.wait(3)
+        here = self.out.at[self.p.c]
+        self.wp = self.l.start(here, here, self.p.core_peer())
+
+    def s4(self):
+        self.wp.wait_recv()
+
+    def drain(self):
+        self.wait(0)
+        self.wait(2)
 
 
 def small_scratch():
@@ -191,21 +256,18 @@
 def big_scratch():
     return [
         pltpu.VMEM((ROWS, WIDE), F32),
-        pltpu.VMEM((2, ROWS, WIDE), BF16),
-        pltpu.VMEM((PACK - 1, QUARTER, WIDE), BF16),
-        pltpu.VMEM((QUARTER, WIDE), F32),
-        pltpu.VMEM((QUARTER, WIDE), BF16),
-        pltpu.VMEM((FRAMES - 1, QUARTER, WIDE), BF16),
+        pltpu.VMEM((ROWS, WIDE), BF16),
+        pltpu.VMEM((ROWS, WIDE), BF16),
+        pltpu.VMEM((ROWS, WIDE), BF16),
+        pltpu.VMEM((CHIPS - 1, PIECE, WIDE), BF16),
+        pltpu.VMEM((FRAMES, PIECE, WIDE), F32),
+        pltpu.VMEM((FRAMES, PIECE, WIDE), BF16),
         pltpu.VMEM((2, ROWS, WIDE), BF16),
     ]
 
 
-COPIES = 2 * (PACK - 1 + FRAMES - 1) + 2 * GROUPS * (2 * (PACK - 1) + FRAMES - 1)
+COPIES = 2 * (PACK - 1 + FRAMES - 1) + 2 * 2
 SPANS = ((1024, 1664), (1664, 2304), (2304, 2816), (2816, COLS), (0, 640), (640, 1024))
-
-
-def row_of(h):
-    return slice(h * HEAD, (h + 1) * HEAD)
 
 
 def in_head(rows):
@@ -218,10 +280,10 @@
 def kernel(
     x_hbm, w_hbm, clip_hbm, og_hbm, att_hbm, ig_hbm,
     xv, wv, clipv, og, feat, ng, inv, dgs, grads, acc, outv, attv, ncol, dcol,
-    lsem, send, recv, *rest,
+    lsem, send, recv, ssem, gsem, *rest,
 ):
     ns, ds_ = rest[:5], rest[5:10]
-    bigs = [rest[10 + 7 * i : 17 + 7 * i] for i in range(2 * GROUPS)]
+    bs, bg = rest[10:18], rest[18:26]
     p = Place()
     barrier = pltpu.get_barrier_semaphore()
     peers = p.peers()
@@ -241,8 +303,8 @@
     links = Links(send, recv)
     norm = Small(p, links, ns, False)
     dnorm = Small(p, links, ds_, True)
-    state = [Big(p, links, bigs[g], False) for g in range(GROUPS)]
-    grad = [Big(p, links, bigs[GROUPS + g], True) for g in range(GROUPS)]
+    state = Big(p, links, bs, ssem, False)
+    grad = Big(p, links, bg, gsem, True)
 
     def project(lo, hi):
         r = tn(wv[:, lo:hi], xv[...])
@@ -252,7 +314,7 @@
         if pos < hi - lo:
             feat[lo + pos : hi, :] = r[pos:].astype(BF16)
 
-    for b in state + grad:
+    for b in (state, grad):
         b.clear()
     loads["clip"].wait()
     is1 = clipv[...] > 0
@@ -290,11 +352,13 @@
         side = jnp.concatenate([m0b, m1b, jnp.zeros((14, TOK), BF16)], axis=0)
         put_rows(norm.own, nt(side, feat[HD : 2 * HD, :]))
 
-    def state_local(g):
-        for i in range(PER):
-            h = g * PER + i
-            k, v = feat[row_of(HEADS + h), :], feat[row_of(2 * HEADS + h), :]
-            state[g].put(i, nt(split(k), v))
+    def put_all(big, terms):
+        last = jnp.concatenate([terms(HEADS - 1), jnp.zeros((2 * HEAD, SPARE), F32)], axis=1)
+        for h in range(HEADS - 1):
+            big.put(h, terms(h), last)
+
+    def state_local():
+        put_all(state, lambda h: nt(split(feat[row_of(HEADS + h), :]), feat[row_of(2 * HEADS + h), :]))
 
     def denominators():
         rows = get_rows(norm.out)[:, :HD]
@@ -306,18 +370,18 @@
         inv[...] = 1.0 / (jnp.where(is1, den[16:], den[:16]) + EPS)
         columns(norm.out, ncol)
 
-    def grad_local(g):
-        for i in range(PER):
-            h = g * PER + i
+    def grad_local():
+        def terms(h):
             v = (og[row_of(h), :].astype(F32) * inv[h : h + 1, :]).astype(BF16)
             ng[row_of(h), :] = v
-            grad[g].put(i, nt(split(feat[row_of(h), :]), v))
-
-    def attend(g):
-        for i in range(PER):
-            h = g * PER + i
+            return nt(split(feat[row_of(h), :]), v)
+
+        put_all(grad, terms)
+
+    def attend():
+        for h in range(HEADS):
             q = feat[row_of(h), :]
-            s0, s1 = state[g].pair(i)
+            s0, s1 = state.pair(h)
             r = inv[h : h + 1, :]
             att = tn(jnp.concatenate([s0, s1], axis=0), split(q))[:HEAD] * r
             attv[row_of(h), :] = att.astype(BF16)
@@ -340,17 +404,15 @@
         ]
         put_rows(dnorm.own, jnp.concatenate(rows, axis=0))
 
-    def value_grads(g):
-        for i in range(PER):
-            h = g * PER + i
-            g0, g1 = grad[g].pair(i)
+    def value_grads():
+        for h in range(HEADS):
+            g0, g1 = grad.pair(h)
             r = tn(jnp.concatenate([g0, g1], axis=0), split(feat[row_of(HEADS + h), :]))
             grads[row_of(2 * HEADS + h), :] = r[:HEAD].astype(BF16)
 
-    def key_grads(g):
-        for i in range(PER):
-            h = g * PER + i
-            g0, g1 = grad[g].pair(i)
+    def key_grads():
+        for h in range(HEADS):
+            g0, g1 = grad.pair(h)
             v = feat[row_of(2 * HEADS + h), :]
             kg = nn(jnp.concatenate([g0, g1], axis=1), split(v, WIDE - HEAD)) + pick(dcol, h)
             keep = feat[row_of(HEADS + h), :].astype(F32) > 0
@@ -390,51 +452,42 @@
     loads[640].start()
     loads["og"].start()
     project(2304, 2816)
-    state_local(0)
-    state[0].s0()
     loads[2816].wait()
     project(2816, COLS)
+    state_local()
+    state.s0()
     norm.s1()
-    state_local(1)
-    state[1].s0()
     loads[0].wait()
     project(0, 640)
-    state[0].s1()
+    state.s1()
     loads[640].wait()
     project(640, 1024)
+    loads["og"].wait()
     norm.s2()
-    loads["og"].wait()
     denominators()
-    grad_local(0)
-    grad[0].s0()
-    state[1].s1()
-    grad_local(1)
-    grad[1].s0()
-    state[0].s2()
-    grad[0].s1()
-    state[1].s2()
-    grad[1].s1()
-    state[0].s3()
-    attend(0)
-    grad[0].s2()
-    state[1].s3()
-    attend(1)
+    grad_local()
+    grad.s0()
+    state.s2()
+    grad.s1()
+    state.s3()
+    grad.s2()
+    state.s4()
+    attend()
     dnorm_local()
     dnorm.s0()
     store(attv, att_hbm.at[0], 0)
-    grad[1].s2()
     back(0, 1024, 0)
     dnorm.s1()
-    grad[0].s3()
-    value_grads(0)
-    grad[1].s3()
-    value_grads(1)
+    grad.s3()
+    grad.s4()
+    value_grads()
     back(2304, COLS, 1)
     dnorm.s2()
     columns(dnorm.out, dcol)
-    key_grads(0)
-    key_grads(1)
+    key_grads()
     back(1024, 2304, 2, lambda m, rows: store(outv.at[rows, :], ig_hbm.at[0, rows, :], 1 + m))
+    state.drain()
+    grad.drain()
     links.drain()
     for s in stores:
         s.wait()
@@ -442,7 +495,6 @@
 
 def per_device(inputs, weight, clip_of_row, out_grad):
     anywhere = pl.BlockSpec(memory_space=pl.ANY)
-    bigs = [r for _ in range(2 * GROUPS) for r in big_scratch()]
     att, grad = pl.pallas_call(
         kernel,
         out_shape=(
@@ -469,9 +521,12 @@
             pltpu.SemaphoreType.DMA((9,)),
             pltpu.SemaphoreType.DMA((COPIES,)),
             pltpu.SemaphoreType.DMA((COPIES,)),
+            pltpu.SemaphoreType.DMA((4,)),
+            pltpu.SemaphoreType.DMA((4,)),
             *small_scratch(),
             *small_scratch(),
-            *bigs,
+            *big_scratch(),
+            *big_scratch(),
         ],
         compiler_params=pltpu.CompilerParams(
             collective_id=0, has_side_effects=True, vmem_limit_bytes=67000000

time: 69.4 us -> 58.7 us (0.85)
  Pallas kernels: 64.1 us -> 54.1 us
    pallas_call x1, Pallas kernels: 64.1 us -> 54.1 us  [per_device(): pl.pallas_call(kernel, out_shape=(jax.ShapeDtypeStruct((1, HD, TOK), BF16...]
where the time goes in v4:
time: 58.7 us; the launch traced here: 58.6 us
  Pallas kernels  54.1 us (92%)
  local copies, waits for them, and re-layouts  3.87 us (7%)
  between operations  0.65 us (1%)
    pallas_call x1, Pallas kernels, per_device(): pl.pallas_call(kernel, out_shape=(jax.ShapeDtypeStruct((1, HD, TOK), BF16...  54.1 us
    unnamed x4, local copies, waits for them, and re-layouts  3.87 us

profile of v4, /device:TPU:1, one launch (start us, length us, event | category | flops | bytes accessed | tf_op | source)
XLA Modules:
  0.0 58.6 jit_solution(7686830046953298590)
XLA Ops:
  0.6 54.1 %shard_map.59 = (bf16[1,1120,512]{2,1,0:T(8,128)(2,1)}, bf16[1,2240,512]{2,1,0:T(8,128)(2,1)}) custom-call(bf16[1,2240,512]{2,1,0:T(8,128)(2,1)} %bitcast.5, bf16[2240,3360]{1,0:T(8,128)(2,1)} %w_hbm.1, s32[1,512]{1,0:T(1,128)} %clip_hbm.1, bf16[1,1120,512]{2,1,0:T(8,128)(2,1)} %bitcast.6), custom_call_target="tpu_custom_call" | custom-call | tf_op jit(solution)/shard_map/pallas_call | solution.py:498
  54.7 0.0 copy-start
  54.7 2.5 %copy.8 = bf16[1,512,1120]{1,2,0:T(8,128)(2,1)} copy(bf16[1,512,1120]{1,2,0:T(8,128)(2,1)} %bitcast.7) | data formatting | bytes 2293760
  57.2 0.0 copy-done
  57.2 1.4 %copy.9 = bf16[1,512,2240]{1,2,0:T(8,128)(2,1)} copy(bf16[1,512,2240]{1,2,0:T(8,128)(2,1)S(1)} %bitcast.4) | data formatting | bytes 4587520
Async XLA Ops:
  54.7 2.5 %copy-start = (bf16[1,2240,512]{2,1,0:T(8,128)(2,1)S(1)}, bf16[1,2240,512]{2,1,0:T(8,128)(2,1)}, u32[]{:S(2)}) copy-start(bf16[1,2240,512]{2,1,0:T(8,128)(2,1)} %get-tuple-element.5) | copy-start | bytes 6881284

commit v5 on v4

--- a/solution.py
+++ b/solution.py
@@ -43,21 +43,35 @@
     return slice(h * HEAD, (h + 1) * HEAD)
 
 
+def hops(e):
+    return sum(min(d, RING - d) for d in (e // FRAMES, (e % FRAMES) // RING, e % RING))
+
+
+FAR_FIRST = sorted(range(1, CHIPS), key=lambda e: (-hops(e), e))
+
+
 class Place:
     def __init__(self):
         self.frame = lax.axis_index("frame")
         self.pack = lax.axis_index("pack")
-        self.x, self.y = self.frame // RING, self.frame % RING
-        self.z, self.c = self.pack // 2, self.pack % 2
+        x, y = lax.div(self.frame, RING), lax.rem(self.frame, RING)
+        z, c = lax.div(self.pack, 2), lax.rem(self.pack, 2)
+        self.z, self.c = z, c
+        self.cs = [c, 1 - c]
+        self.zs = [z] + [lax.rem(z + d, RING) for d in range(1, RING)]
+        self.ahead = self.grid(x, y, 1)
+        self.behind = self.grid(x, y, RING - 1)
+
+    def grid(self, x, y, step):
+        xs = [lax.rem(x + step * d, RING) * RING for d in range(RING)]
+        ys = [lax.rem(y + step * d, RING) for d in range(RING)]
+        return [u + v for u in xs for v in ys]
 
     def core_peer(self):
         return self.pack_peer(0)
 
-    def chip(self, e, sign=1):
-        dz, dx, dy = e // FRAMES, (e % FRAMES) // RING, e % RING
-        x = (self.x + sign * dx + RING) % RING
-        y = (self.y + sign * dy + RING) % RING
-        return x * RING + y, (self.z + sign * dz + RING) % RING
+    def chip(self, e):
+        return self.ahead[e % FRAMES], self.zs[e // FRAMES]
 
     def chip_peer(self, e):
         frame, z = self.chip(e)
@@ -65,12 +79,10 @@
 
     def pack_peer(self, k):
         dz, flip = divmod(k + 1, 2)
-        z = (self.z + dz) % RING
-        c = (self.c + flip) % 2
-        return {"frame": self.frame, "pack": z * 2 + c}
+        return {"frame": self.frame, "pack": self.zs[dz] * 2 + self.cs[flip]}
 
     def frame_peer(self, j):
-        return {"frame": (self.frame + j + FRAMES) % FRAMES, "pack": self.pack}
+        return {"frame": lax.rem(self.frame + (j % FRAMES), FRAMES), "pack": self.pack}
 
     def peers(self):
         other = [self.pack_peer(k) for k in range(0, PACK - 1, 2)]
@@ -215,7 +227,7 @@
         total = self.acc[...] + self.rc[...].astype(F32)
         self.acc[...] = total
         self.sz[...] = total.astype(BF16)
-        for e in range(1, CHIPS):
+        for e in FAR_FIRST:
             frame, z = self.p.chip(e)
             self.send(0, self.sz.at[self.piece(z * FRAMES + frame), :], self.rz.at[e - 1], self.p.chip_peer(e))
 
@@ -225,14 +237,14 @@
             total = self.acc[self.mine(), :] if d == 0 else self.rz[d - 1].astype(F32)
             for dz in range(1, RING):
                 total = total + self.rz[dz * FRAMES + d - 1].astype(F32)
-            self.blocks[self.p.chip(d, -1)[0]] = total
+            self.blocks[self.p.behind[d]] = total
         total = jnp.zeros((PIECE, WIDE), F32)
         for f in reversed(range(FRAMES)) if self.reverse else range(FRAMES):
             total = total + self.blocks[f]
             self.sums[f] = total.astype(BF16)
         here = self.out.at[self.p.c, self.mine(), :]
         here[...] = self.sums[self.p.frame]
-        for e in range(1, CHIPS):
+        for e in FAR_FIRST:
             self.send(1, self.sums.at[self.p.chip(e)[0]], here, self.p.chip_peer(e))
 
     def s3(self):
@@ -278,8 +290,8 @@
 
 
 def kernel(
-    x_hbm, w_hbm, clip_hbm, og_hbm, att_hbm, ig_hbm,
-    xv, wv, clipv, og, feat, ng, inv, dgs, grads, acc, outv, attv, ncol, dcol,
+    x_hbm, w_hbm, clip_hbm, og_hbm, attv, outv,
+    xv, wv, clipv, og, feat, ng, inv, dgs, grads, acc, ncol, dcol,
     lsem, send, recv, ssem, gsem, *rest,
 ):
     ns, ds_ = rest[:5], rest[5:10]
@@ -287,9 +299,6 @@
     p = Place()
     barrier = pltpu.get_barrier_semaphore()
     peers = p.peers()
-    for peer in peers:
-        pl.semaphore_signal(barrier, inc=1, device_id=peer, device_id_type=MESH)
-
     loads = {
         "clip": pltpu.make_async_copy(clip_hbm, clipv, lsem.at[0]),
         "x": pltpu.make_async_copy(x_hbm.at[0], xv, lsem.at[1]),
@@ -297,8 +306,10 @@
     }
     for i, (lo, hi) in enumerate(SPANS):
         loads[lo] = pltpu.make_async_copy(w_hbm.at[:, lo:hi], wv.at[:, lo:hi], lsem.at[3 + i])
-    for name in ("clip", "x", 1024):
+    for name in ("x", 1024, "clip"):
         loads[name].start()
+    for peer in peers:
+        pl.semaphore_signal(barrier, inc=1, device_id=peer, device_id_type=MESH)
 
     links = Links(send, recv)
     norm = Small(p, links, ns, False)
@@ -384,7 +395,7 @@
             s0, s1 = state.pair(h)
             r = inv[h : h + 1, :]
             att = tn(jnp.concatenate([s0, s1], axis=0), split(q))[:HEAD] * r
-            attv[row_of(h), :] = att.astype(BF16)
+            attv[0, row_of(h), :] = att.astype(BF16)
             d = -jnp.sum(og[row_of(h), :].astype(F32) * att, axis=0, keepdims=True) * r
             dgs[h : h + 1, :] = d
             qg = nn(jnp.concatenate([s0, s1], axis=1), split(ng[row_of(h), :], WIDE - HEAD))
@@ -418,7 +429,7 @@
             keep = feat[row_of(HEADS + h), :].astype(F32) > 0
             grads[row_of(HEADS + h), :] = jnp.where(keep, kg, 0.0).astype(BF16)
 
-    def back(lo, hi, kind, then=None):
+    def back(lo, hi, kind):
         for m in (0, 1):
             rows = slice(m * HD, (m + 1) * HD)
             r = nn(wv[rows, lo:hi], grads[lo:hi, :])
@@ -427,14 +438,7 @@
             if kind < 2:
                 acc[rows, :] = r
             else:
-                outv[rows, :] = r.astype(BF16)
-                then(m, rows)
-
-    stores = []
-
-    def store(src, dst, at):
-        stores.append(pltpu.make_async_copy(src, dst, lsem.at[at]))
-        stores[-1].start()
+                outv[0, rows, :] = r.astype(BF16)
 
     loads["x"].wait()
     loads[1024].wait()
@@ -454,12 +458,13 @@
     project(2304, 2816)
     loads[2816].wait()
     project(2816, COLS)
+    norm.s1()
     state_local()
     state.s0()
-    norm.s1()
     loads[0].wait()
-    project(0, 640)
+    project(0, 256)
     state.s1()
+    project(256, 640)
     loads[640].wait()
     project(640, 1024)
     loads["og"].wait()
@@ -475,7 +480,6 @@
     attend()
     dnorm_local()
     dnorm.s0()
-    store(attv, att_hbm.at[0], 0)
     back(0, 1024, 0)
     dnorm.s1()
     grad.s3()
@@ -485,24 +489,19 @@
     dnorm.s2()
     columns(dnorm.out, dcol)
     key_grads()
-    back(1024, 2304, 2, lambda m, rows: store(outv.at[rows, :], ig_hbm.at[0, rows, :], 1 + m))
+    back(1024, 2304, 2)
     state.drain()
     grad.drain()
     links.drain()
-    for s in stores:
-        s.wait()
 
 
 def per_device(inputs, weight, clip_of_row, out_grad):
     anywhere = pl.BlockSpec(memory_space=pl.ANY)
     att, grad = pl.pallas_call(
         kernel,
-        out_shape=(
-            jax.ShapeDtypeStruct((1, HD, TOK), BF16),
-            jax.ShapeDtypeStruct((1, D, TOK), BF16),
-        ),
+        out_shape=(pltpu.VMEM((1, HD, TOK), BF16), pltpu.VMEM((1, D, TOK), BF16)),
         in_specs=[anywhere] * 4,
-        out_specs=(anywhere, anywhere),
+        out_specs=(pl.BlockSpec(memory_space=pltpu.VMEM),) * 2,
         scratch_shapes=[
             pltpu.VMEM((D, TOK), BF16),
             pltpu.VMEM((D, COLS), BF16),
@@ -514,8 +513,6 @@
             pltpu.VMEM((16, TOK), F32),
             pltpu.VMEM((COLS, TOK), BF16),
             pltpu.VMEM((D, TOK), F32),
-            pltpu.VMEM((D, TOK), BF16),
-            pltpu.VMEM((HD, TOK), BF16),
             pltpu.VMEM((TILES * WIDE, 8), F32),
             pltpu.VMEM((TILES * WIDE, 8), F32),
             pltpu.SemaphoreType.DMA((9,)),
@@ -529,7 +526,7 @@
             *big_scratch(),
         ],
         compiler_params=pltpu.CompilerParams(
-            collective_id=0, has_side_effects=True, vmem_limit_bytes=67000000
+            collective_id=0, has_side_effects=True, vmem_limit_bytes=54000000
         ),
     )(inputs.swapaxes(1, 2), weight, clip_of_row, out_grad.swapaxes(1, 2))
     return att.swapaxes(1, 2), grad.swapaxes(1, 2)

time: 58.7 us -> 54.4 us (0.927)
  Pallas kernels: 54.1 us -> 51.3 us
  local copies, waits for them, and re-layouts: 3.87 us -> 2.39 us
    pallas_call x1, Pallas kernels: 54.1 us -> 51.3 us  [per_device(): pl.pallas_call(kernel, out_shape=(pltpu.VMEM((1, HD, TOK), BF16), pltpu.V...]
    unnamed x4 -> x2, local copies, waits for them, and re-layouts: 3.87 us -> 2.39 us
where the time goes in v5:
time: 54.4 us; the launch traced here: 54.3 us
  Pallas kernels  51.3 us (94%)
  local copies, waits for them, and re-layouts  2.39 us (4%)
  between operations  0.64 us (1%)
    pallas_call x1, Pallas kernels, per_device(): pl.pallas_call(kernel, out_shape=(pltpu.VMEM((1, HD, TOK), BF16), pltpu.V...  51.3 us
    unnamed x2, local copies, waits for them, and re-layouts  2.39 us

profile of v5, /device:TPU:1, one launch (start us, length us, event | category | flops | bytes accessed | tf_op | source)
XLA Modules:
  0.0 54.3 jit_solution(14900643045059096400)
XLA Ops:
  0.6 51.3 %shard_map.59 = (bf16[1,1120,512]{2,1,0:T(8,128)(2,1)S(1)}, bf16[1,2240,512]{2,1,0:T(8,128)(2,1)S(1)}) custom-call(bf16[1,2240,512]{2,1,0:T(8,128)(2,1)} %bitcast.6, bf16[2240,3360]{1,0:T(8,128)(2,1)} %w_hbm.1, s32[1,512]{1,0:T(1,128)} %clip_hbm.1, bf16[1,1120,512]{2,1,0:T(8,128)(2,1)} %bitcast.7), custom_call_target="tpu_custom_call" | custom-call | tf_op jit(solution)/shard_map/pallas_call | solution.py:500
  51.9 1.0 %copy.8 = bf16[1,512,1120]{1,2,0:T(8,128)(2,1)} copy(bf16[1,512,1120]{1,2,0:T(8,128)(2,1)S(1)} %bitcast.5) | data formatting | bytes 2293760
  52.9 1.4 %copy.9 = bf16[1,512,2240]{1,2,0:T(8,128)(2,1)} copy(bf16[1,512,2240]{1,2,0:T(8,128)(2,1)S(1)} %bitcast.4) | data formatting | bytes 4587520

commit v6 on v5

--- a/solution.py
+++ b/solution.py
@@ -85,8 +85,10 @@
         return {"frame": lax.rem(self.frame + (j % FRAMES), FRAMES), "pack": self.pack}
 
     def peers(self):
-        other = [self.pack_peer(k) for k in range(0, PACK - 1, 2)]
-        return other + [self.chip_peer(e) for e in range(1, CHIPS)]
+        return [self.pack_peer(k) for k in range(PACK - 1)] + self.frame_peers()
+
+    def frame_peers(self):
+        return [self.frame_peer(j) for j in range(1, FRAMES)]
 
 
 class Links:
@@ -292,7 +294,7 @@
 def kernel(
     x_hbm, w_hbm, clip_hbm, og_hbm, attv, outv,
     xv, wv, clipv, og, feat, ng, inv, dgs, grads, acc, ncol, dcol,
-    lsem, send, recv, ssem, gsem, *rest,
+    lsem, send, recv, ssem, gsem, entry, *rest,
 ):
     ns, ds_ = rest[:5], rest[5:10]
     bs, bg = rest[10:18], rest[18:26]
@@ -452,6 +454,8 @@
     norm_local()
     pl.semaphore_wait(barrier, len(peers))
     norm.s0()
+    for peer in p.frame_peers():
+        pl.semaphore_signal(entry, inc=1, device_id=peer, device_id_type=MESH)
     loads[2304].wait()
     loads[640].start()
     loads["og"].start()
@@ -463,6 +467,7 @@
     state.s0()
     loads[0].wait()
     project(0, 256)
+    pl.semaphore_wait(entry, FRAMES - 1)
     state.s1()
     project(256, 640)
     loads[640].wait()
@@ -472,17 +477,17 @@
     denominators()
     grad_local()
     grad.s0()
+    grad.s1()
     state.s2()
-    grad.s1()
+    grad.s2()
     state.s3()
-    grad.s2()
     state.s4()
     attend()
     dnorm_local()
     dnorm.s0()
     back(0, 1024, 0)
+    grad.s3()
     dnorm.s1()
-    grad.s3()
     grad.s4()
     value_grads()
     back(2304, COLS, 1)
@@ -520,6 +525,7 @@
             pltpu.SemaphoreType.DMA((COPIES,)),
             pltpu.SemaphoreType.DMA((4,)),
             pltpu.SemaphoreType.DMA((4,)),
+            pltpu.SemaphoreType.REGULAR,
             *small_scratch(),
             *small_scratch(),
             *big_scratch(),

time: 54.4 us -> 51.8 us (0.952)
  Pallas kernels: 51.3 us -> 48.4 us
    pallas_call x1, Pallas kernels: 51.3 us -> 48.4 us  [per_device(): pl.pallas_call(kernel, out_shape=(pltpu.VMEM((1, HD, TOK), BF16), pltpu.V...]
where the time goes in v6:
time: 51.8 us; the launch traced here: 51.4 us
  Pallas kernels  48.4 us (93%)
  local copies, waits for them, and re-layouts  2.39 us (5%)
  between operations  0.64 us (1%)
    pallas_call x1, Pallas kernels, per_device(): pl.pallas_call(kernel, out_shape=(pltpu.VMEM((1, HD, TOK), BF16), pltpu.V...  48.4 us
    unnamed x2, local copies, waits for them, and re-layouts  2.39 us

profile of v6, /device:TPU:1, one launch (start us, length us, event | category | flops | bytes accessed | tf_op | source)
XLA Modules:
  0.0 51.4 jit_solution(12797714620965176761)
XLA Ops:
  0.6 48.4 %shard_map.59 = (bf16[1,1120,512]{2,1,0:T(8,128)(2,1)S(1)}, bf16[1,2240,512]{2,1,0:T(8,128)(2,1)S(1)}) custom-call(bf16[1,2240,512]{2,1,0:T(8,128)(2,1)} %bitcast.6, bf16[2240,3360]{1,0:T(8,128)(2,1)} %w_hbm.1, s32[1,512]{1,0:T(1,128)} %clip_hbm.1, bf16[1,1120,512]{2,1,0:T(8,128)(2,1)} %bitcast.7), custom_call_target="tpu_custom_call" | custom-call | tf_op jit(solution)/shard_map/pallas_call | solution.py:505
  49.0 1.0 %copy.8 = bf16[1,512,1120]{1,2,0:T(8,128)(2,1)} copy(bf16[1,512,1120]{1,2,0:T(8,128)(2,1)S(1)} %bitcast.5) | data formatting | bytes 2293760
  50.0 1.4 %copy.9 = bf16[1,512,2240]{1,2,0:T(8,128)(2,1)} copy(bf16[1,512,2240]{1,2,0:T(8,128)(2,1)S(1)} %bitcast.4) | data formatting | bytes 4587520

commit v7 on v6

--- a/solution.py
+++ b/solution.py
@@ -127,16 +127,16 @@
     def spread(self, src, slots):
         f = self.p.frame
         self.w = []
-        for j in range(1, FRAMES):
+        for j in sorted(range(1, FRAMES), key=lambda j: (-hops(j), j)):
             to, into = (f >= j, f + j < FRAMES) if self.reverse else (f + j < FRAMES, f >= j)
             peer = self.p.frame_peer(-j if self.reverse else j)
-            self.w.append((self.l.start(src, slots.at[j - 1], peer, to), into))
+            self.w.append((self.l.start(src, slots.at[j - 1], peer, to), into, j - 1))
 
     def total(self, own, slots):
-        for copy, into in self.w:
+        for copy, into, _ in self.w:
             pl.when(into)(copy.wait_recv)
-        for j, (_, into) in enumerate(self.w):
-            own = own + jnp.where(into, slots[j].astype(F32), 0.0)
+        for _, into, slot in self.w:
+            own = own + jnp.where(into, slots[slot], 0.0)
         return own
 
 
@@ -281,7 +281,7 @@
 
 
 COPIES = 2 * (PACK - 1 + FRAMES - 1) + 2 * 2
-SPANS = ((1024, 1664), (1664, 2304), (2304, 2816), (2816, COLS), (0, 640), (640, 1024))
+SPANS = ((1024, 1408), (1408, 2304), (2304, COLS), (0, 256), (256, 1024))
 
 
 def in_head(rows):
@@ -444,34 +444,30 @@
 
     loads["x"].wait()
     loads[1024].wait()
-    loads[1664].start()
+    loads[1408].start()
     loads[2304].start()
-    project(1024, 1664)
-    loads[1664].wait()
-    loads[2816].start()
+    project(1024, 1408)
+    loads[1408].wait()
     loads[0].start()
-    project(1664, 2304)
+    loads[256].start()
+    project(1408, 2304)
     norm_local()
     pl.semaphore_wait(barrier, len(peers))
     norm.s0()
     for peer in p.frame_peers():
         pl.semaphore_signal(entry, inc=1, device_id=peer, device_id_type=MESH)
     loads[2304].wait()
-    loads[640].start()
     loads["og"].start()
-    project(2304, 2816)
-    loads[2816].wait()
-    project(2816, COLS)
-    norm.s1()
+    project(2304, COLS)
     state_local()
     state.s0()
+    norm.s1()
     loads[0].wait()
     project(0, 256)
     pl.semaphore_wait(entry, FRAMES - 1)
     state.s1()
-    project(256, 640)
-    loads[640].wait()
-    project(640, 1024)
+    loads[256].wait()
+    project(256, 1024)
     loads["og"].wait()
     norm.s2()
     denominators()
@@ -520,7 +516,7 @@
             pltpu.VMEM((D, TOK), F32),
             pltpu.VMEM((TILES * WIDE, 8), F32),
             pltpu.VMEM((TILES * WIDE, 8), F32),
-            pltpu.SemaphoreType.DMA((9,)),
+            pltpu.SemaphoreType.DMA((8,)),
             pltpu.SemaphoreType.DMA((COPIES,)),
             pltpu.SemaphoreType.DMA((COPIES,)),
             pltpu.SemaphoreType.DMA((4,)),

time: 51.8 us -> 52.1 us (level)
  Pallas kernels: 48.4 us -> 49 us
    pallas_call x1, Pallas kernels: 48.4 us -> 49 us  [per_device(): pl.pallas_call(kernel, out_shape=(pltpu.VMEM((1, HD, TOK), BF16), pltpu.V...]
where the time goes in v7:
time: 52.1 us; the launch traced here: 52 us
  Pallas kernels  49 us (94%)
  local copies, waits for them, and re-layouts  2.39 us (5%)
  between operations  0.64 us (1%)
    pallas_call x1, Pallas kernels, per_device(): pl.pallas_call(kernel, out_shape=(pltpu.VMEM((1, HD, TOK), BF16), pltpu.V...  49 us
    unnamed x2, local copies, waits for them, and re-layouts  2.39 us

profile of v7, /device:TPU:1, one launch (start us, length us, event | category | flops | bytes accessed | tf_op | source)
XLA Modules:
  0.0 52.0 jit_solution(11862114713309562501)
XLA Ops:
  0.6 49.0 %shard_map.59 = (bf16[1,1120,512]{2,1,0:T(8,128)(2,1)S(1)}, bf16[1,2240,512]{2,1,0:T(8,128)(2,1)S(1)}) custom-call(bf16[1,2240,512]{2,1,0:T(8,128)(2,1)} %bitcast.6, bf16[2240,3360]{1,0:T(8,128)(2,1)} %w_hbm.1, s32[1,512]{1,0:T(1,128)} %clip_hbm.1, bf16[1,1120,512]{2,1,0:T(8,128)(2,1)} %bitcast.7), custom_call_target="tpu_custom_call" | custom-call | tf_op jit(solution)/shard_map/pallas_call | solution.py:501
  49.6 1.0 %copy.8 = bf16[1,512,1120]{1,2,0:T(8,128)(2,1)} copy(bf16[1,512,1120]{1,2,0:T(8,128)(2,1)S(1)} %bitcast.5) | data formatting | bytes 2293760
  50.6 1.4 %copy.9 = bf16[1,512,2240]{1,2,0:T(8,128)(2,1)} copy(bf16[1,512,2240]{1,2,0:T(8,128)(2,1)S(1)} %bitcast.4) | data formatting | bytes 4587520

commit v8 on v7

--- a/solution.py
+++ b/solution.py
@@ -459,9 +459,9 @@
     loads[2304].wait()
     loads["og"].start()
     project(2304, COLS)
+    norm.s1()
     state_local()
     state.s0()
-    norm.s1()
     loads[0].wait()
     project(0, 256)
     pl.semaphore_wait(entry, FRAMES - 1)
@@ -482,8 +482,8 @@
     dnorm_local()
     dnorm.s0()
     back(0, 1024, 0)
+    dnorm.s1()
     grad.s3()
-    dnorm.s1()
     grad.s4()
     value_grads()
     back(2304, COLS, 1)

time: 52.1 us -> 53.2 us (1.021)
  Pallas kernels: 49 us -> 50.1 us
    pallas_call x1, Pallas kernels: 49 us -> 50.1 us  [per_device(): pl.pallas_call(kernel, out_shape=(pltpu.VMEM((1, HD, TOK), BF16), pltpu.V...]
where the time goes in v8:
time: 53.2 us; the launch traced here: 53.1 us
  Pallas kernels  50.1 us (94%)
  local copies, waits for them, and re-layouts  2.39 us (4%)
  between operations  0.64 us (1%)
    pallas_call x1, Pallas kernels, per_device(): pl.pallas_call(kernel, out_shape=(pltpu.VMEM((1, HD, TOK), BF16), pltpu.V...  50.1 us
    unnamed x2, local copies, waits for them, and re-layouts  2.39 us

profile of v8, /device:TPU:1, one launch (start us, length us, event | category | flops | bytes accessed | tf_op | source)
XLA Modules:
  0.0 53.1 jit_solution(14293153177285629894)
XLA Ops:
  0.6 50.1 %shard_map.59 = (bf16[1,1120,512]{2,1,0:T(8,128)(2,1)S(1)}, bf16[1,2240,512]{2,1,0:T(8,128)(2,1)S(1)}) custom-call(bf16[1,2240,512]{2,1,0:T(8,128)(2,1)} %bitcast.6, bf16[2240,3360]{1,0:T(8,128)(2,1)} %w_hbm.1, s32[1,512]{1,0:T(1,128)} %clip_hbm.1, bf16[1,1120,512]{2,1,0:T(8,128)(2,1)} %bitcast.7), custom_call_target="tpu_custom_call" | custom-call | tf_op jit(solution)/shard_map/pallas_call | solution.py:501
  50.7 1.0 %copy.8 = bf16[1,512,1120]{1,2,0:T(8,128)(2,1)} copy(bf16[1,512,1120]{1,2,0:T(8,128)(2,1)S(1)} %bitcast.5) | data formatting | bytes 2293760
  51.7 1.4 %copy.9 = bf16[1,512,2240]{1,2,0:T(8,128)(2,1)} copy(bf16[1,512,2240]{1,2,0:T(8,128)(2,1)S(1)} %bitcast.4) | data formatting | bytes 4587520

commit v9 on v8

--- a/solution.py
+++ b/solution.py
@@ -482,8 +482,8 @@
     dnorm_local()
     dnorm.s0()
     back(0, 1024, 0)
+    grad.s3()
     dnorm.s1()
-    grad.s3()
     grad.s4()
     value_grads()
     back(2304, COLS, 1)

time: 53.2 us -> 52.1 us (0.979)
  Pallas kernels: 50.1 us -> 48.9 us
    pallas_call x1, Pallas kernels: 50.1 us -> 48.9 us  [per_device(): pl.pallas_call(kernel, out_shape=(pltpu.VMEM((1, HD, TOK), BF16), pltpu.V...]
where the time goes in v9:
time: 52.1 us; the launch traced here: 52 us
  Pallas kernels  48.9 us (94%)
  local copies, waits for them, and re-layouts  2.39 us (5%)
  between operations  0.64 us (1%)
    pallas_call x1, Pallas kernels, per_device(): pl.pallas_call(kernel, out_shape=(pltpu.VMEM((1, HD, TOK), BF16), pltpu.V...  48.9 us
    unnamed x2, local copies, waits for them, and re-layouts  2.39 us

profile of v9, /device:TPU:1, one launch (start us, length us, event | category | flops | bytes accessed | tf_op | source)
XLA Modules:
  0.0 52.0 jit_solution(143919913912794335)
XLA Ops:
  0.6 48.9 %shard_map.59 = (bf16[1,1120,512]{2,1,0:T(8,128)(2,1)S(1)}, bf16[1,2240,512]{2,1,0:T(8,128)(2,1)S(1)}) custom-call(bf16[1,2240,512]{2,1,0:T(8,128)(2,1)} %bitcast.6, bf16[2240,3360]{1,0:T(8,128)(2,1)} %w_hbm.1, s32[1,512]{1,0:T(1,128)} %clip_hbm.1, bf16[1,1120,512]{2,1,0:T(8,128)(2,1)} %bitcast.7), custom_call_target="tpu_custom_call" | custom-call | tf_op jit(solution)/shard_map/pallas_call | solution.py:501
  49.6 1.0 %copy.8 = bf16[1,512,1120]{1,2,0:T(8,128)(2,1)} copy(bf16[1,512,1120]{1,2,0:T(8,128)(2,1)S(1)} %bitcast.5) | data formatting | bytes 2293760
  50.6 1.4 %copy.9 = bf16[1,512,2240]{1,2,0:T(8,128)(2,1)} copy(bf16[1,512,2240]{1,2,0:T(8,128)(2,1)S(1)} %bitcast.4) | data formatting | bytes 4587520
